TPU v7x, 768 devices: a whole 4x8x12 slice. The times are simulated.
768 devices in a mesh: walker: 12 (over z), orb: 64 (over x, y, core).
Axes of the slice: x: 4, y: 8, z: 12, core: 2. Of those that a mesh axis runs over, the one named last changes fastest.
Arguments:
- occupations: int32 [3072, 128], P(('walker', 'orb')), may hold values from 0 to 255, as said below
- local_energy: float32 [3072], P(('walker', 'orb')), may hold values from -4.5 to -0.5
- embed_weight: bfloat16 [18, 256], replicated, may hold values from -1.5 to 1.5
- conv_weight: bfloat16 [2304, 256], replicated, may hold values from -0.125 to 0.125
- head_weight: bfloat16 [256, 128], replicated, may hold values from -0.375 to 0.375
- a_factor: float32 [256, 256], P('orb'), may hold values from -1 to 2, as said below
- g_factor: float32 [128, 128], replicated, may hold values from -1 to 2, as said below
- a_inverse: float32 [256, 256], P('orb'), may hold values from -1 to 2, as said below
- g_inverse: float32 [128, 128], replicated, may hold values from -1 to 2, as said below
Outputs:
- head_update: float32 [256, 128], P('orb')
- conv_update: float32 [2304, 256], P('orb')
- new_a_factor: float32 [256, 256], P('orb')
- new_g_factor: float32 [128, 128], replicated
Inputs may be any that keep to these rules, and one draw needn't show every extreme that they name: `occupations`: in each row the first 64 entries are distinct sites, and so are the last 64. `a_factor`: Symmetric; each diagonal entry exceeds the sum of the magnitudes of the other entries of its row. `g_factor`: Symmetric; each diagonal entry exceeds the sum of the magnitudes of the other entries of its row. `a_inverse`: Symmetric; each diagonal entry exceeds the sum of the magnitudes of the other entries of its row. `g_inverse`: Symmetric; each diagonal entry exceeds the sum of the magnitudes of the other entries of its row.
All inputs are finite; a program needn't handle non-finite values.
Results may differ from a plain program's by a relative error of at most 0.0071.
Values sent between devices are 32-bit elements; how exact they have to be, the bound alone decides.
A program may use at most 64 MiB of HBM per device.

v0:
```python
import math

import jax
import jax.numpy as jnp
from jax import lax
from jax.sharding import PartitionSpec as P

L = 16
C = 256
NS_STEPS = 3
NE = 128


decay_rate = 0.8


def neighbours(lattice):
    shifted_views = [
        jnp.roll(lattice, (-shift_x, -shift_y), axis=(1, 2))
        for shift_x in (-1, 0, 1)
        for shift_y in (-1, 0, 1)
    ]
    return jnp.concatenate(shifted_views, axis=-1)


def per_device(
    occupations,
    local_energy,
    embed_weight,
    conv_weight,
    head_weight,
    a_factor,
    g_factor,
    a_inverse,
    g_inverse,
):
    sample_count = occupations.shape[0]
    site_count = L * L
    site_ids = jnp.arange(site_count, dtype=jnp.int32)
    select = (occupations[:, :, None] == site_ids[None, None, :]).astype(jnp.bfloat16)
    half_count = NE // 2
    up_fill = jnp.sum(select[:, :half_count].astype(jnp.float32), axis=1)
    down_fill = jnp.sum(select[:, half_count:].astype(jnp.float32), axis=1)
    lattice = (
        jnp.stack([up_fill, down_fill], axis=-1).reshape(sample_count, L, L, 2).astype(jnp.bfloat16)
    )
    embed_in = neighbours(lattice).reshape(sample_count * site_count, 18)
    embedded = jnp.tanh(jnp.dot(embed_in, embed_weight, preferred_element_type=jnp.float32)).astype(
        jnp.bfloat16
    )
    patches = neighbours(embedded.reshape(sample_count, L, L, C)).reshape(
        sample_count, site_count, 9 * C
    )
    conv_pre = jnp.dot(
        patches.reshape(sample_count * site_count, 9 * C),
        conv_weight,
        preferred_element_type=jnp.float32,
    )
    squash = jnp.tanh(conv_pre)
    hidden = (
        (embedded.astype(jnp.float32) + squash)
        .astype(jnp.bfloat16)
        .reshape(sample_count, site_count, C)
    )
    electron_rows = jnp.einsum(
        "bis,bsc->bic", select, hidden, preferred_element_type=jnp.float32
    ).astype(jnp.bfloat16)
    logits = jnp.dot(
        electron_rows.reshape(sample_count * NE, C), head_weight, preferred_element_type=jnp.float32
    ).reshape(sample_count, NE, NE)
    orbital_tanh = jnp.tanh(logits)
    identity = jnp.eye(NE, dtype=jnp.float32)
    slater_scale = 0.35 / math.sqrt(NE)
    slater = identity + slater_scale * orbital_tanh
    inverse_est = jnp.broadcast_to(identity, slater.shape)
    for sweep in range(NS_STEPS):
        product = jnp.einsum("bij,bjk->bik", slater, inverse_est, precision=lax.Precision.HIGHEST)
        inverse_est = jnp.einsum(
            "bij,bjk->bik", inverse_est, 2.0 * identity - product, precision=lax.Precision.HIGHEST
        )
    log_grads = (1.0 - orbital_tanh * orbital_tanh) * jnp.swapaxes(inverse_est, 1, 2)
    cotangent = (slater_scale * log_grads).astype(jnp.bfloat16)
    head_terms = jnp.einsum(
        "bic,bij->bcj", electron_rows, cotangent, preferred_element_type=jnp.float32
    )
    flat_rows = electron_rows.reshape(sample_count * NE, C)
    input_gram = jnp.einsum("nc,nd->cd", flat_rows, flat_rows, preferred_element_type=jnp.float32)
    output_gram = jnp.einsum("bik,bil->kl", log_grads, log_grads, precision=lax.Precision.HIGHEST)
    row_grads = (
        jnp.dot(
            cotangent.reshape(sample_count * NE, NE),
            head_weight.T,
            preferred_element_type=jnp.float32,
        )
        .astype(jnp.bfloat16)
        .reshape(sample_count, NE, C)
    )
    hidden_grad = jnp.einsum("bis,bic->bsc", select, row_grads, preferred_element_type=jnp.float32)
    pre_grad = (
        (hidden_grad.reshape(sample_count * site_count, C) * (1.0 - squash * squash))
        .astype(jnp.bfloat16)
        .reshape(sample_count, site_count, C)
    )
    samples_all = sample_count * lax.axis_size("walker") * lax.axis_size("orb")
    energy_sum = jnp.sum(local_energy)
    energy_whole = lax.psum(energy_sum, ("walker", "orb"))
    mean_energy = energy_whole / samples_all
    weights = (local_energy - mean_energy) / samples_all
    head_part = jnp.sum(weights[:, None, None] * head_terms, axis=0)
    input_sum, output_sum, head_grad = lax.psum(
        (input_gram, output_gram, head_part), ("walker", "orb")
    )
    orb_count = lax.axis_size("orb")
    orb_place = lax.axis_index("orb")
    panel_rows = 9 * C // orb_count
    terms = jnp.einsum("bsk,bsc->bkc", patches, pre_grad, preferred_element_type=jnp.float32)
    conv_full = lax.psum(jnp.sum(weights[:, None, None] * terms, axis=0), ("walker", "orb"))
    conv_panel = lax.dynamic_slice_in_dim(conv_full, orb_place * panel_rows, panel_rows, 0)
    head_rows = C // orb_count
    row_start = orb_place * head_rows
    grad_rows = lax.dynamic_slice_in_dim(head_grad, row_start, head_rows, 0)
    left_applied = jnp.dot(a_inverse, head_grad, precision=lax.Precision.HIGHEST)
    precond_rows = jnp.dot(left_applied, g_inverse, precision=lax.Precision.HIGHEST)
    head_local = jnp.sum(precond_rows * grad_rows)
    conv_local = jnp.sum(conv_panel * conv_panel)
    head_norm, conv_norm = lax.psum((head_local, conv_local), "orb")
    head_update = -jnp.sqrt(C * NE / 4.0 / head_norm) * precond_rows
    conv_update = -jnp.sqrt(9 * C * C / 4.0 / conv_norm) * conv_panel
    input_rows = lax.dynamic_slice_in_dim(input_sum, row_start, head_rows, 0)
    new_a_factor = decay_rate * a_factor + (1.0 - decay_rate) * input_rows / (samples_all * NE)
    new_g_factor = decay_rate * g_factor + (1.0 - decay_rate) * output_sum / samples_all
    return (head_update, conv_update, new_a_factor, new_g_factor)


def solution(mesh):
    in_specs = (
        P(("walker", "orb"), None),
        P(("walker", "orb")),
        P(),
        P(),
        P(),
        P("orb", None),
        P(),
        P("orb", None),
        P(),
    )
    out_specs = (P("orb", None), P("orb", None), P("orb", None), P())
    return jax.shard_map(
        per_device, mesh=mesh, in_specs=in_specs, out_specs=out_specs, check_vma=False
    )
```

profile of v0, /device:TPU:1, one launch (start us, length us, event | category | flops | bytes accessed | tf_op | source)
XLA Modules:
  0.0 818.3 jit_solution(6728591896224830082)
XLA Ops:
  10.5 1.0 fusion
  17.0 2.4 add_convert_fusion
  21.0 1.6 copy.30
  22.6 1.5 convolution_subtract_fusion.2
  24.1 1.5 fusion.15
  25.6 1.5 convolution_subtract_fusion.1
  27.8 1.5 convolution_subtract_fusion
  29.2 1.4 multiply_convert_fusion
  30.8 1.3 fusion.7
  32.1 1.0 copy.34
  33.2 1.9 constant_dynamic-update-slice_fusion.19
  35.1 1.0 copy.35
  36.1 2.1 copy.36
  38.2 2.1 copy.37
  40.3 1.0 copy.38
  41.3 1.0 copy.39
  42.4 2.0 copy.40
  45.2 1.0 copy.42
  46.2 120.6 %psum.49 = f32[]{:T(128)} all-reduce(f32[]{:T(128)} %reduce_sum.63), channel_id=1, replica_groups=mesh['walker'=12,'orb'=64] {'walker','orb'}, use_global_device_ids=true, to_apply=%region_1.0 | all-reduce | flops 1 | bytes 8 | tf_op jit(solution)/shard_map/psum | solution.py:106
  167.6 2.0 fusion.1
  169.6 1.2 convolution_bitcast_fusion.1
  170.8 1.7 fusion.2
  172.5 1.9 constant_dynamic-update-slice_fusion.18
  180.3 5.3 multiply_reduce_fusion
  185.7 488.9 %all-reduce.4.cloned.1.call-done = (f32[256,128]{1,0:T(8,128)}, f32[2304,256]{1,0:T(8,128)}, f32[256,256]{1,0:T(8,128)}, f32[128,128]{1,0:T(8,128)}) async-done(((f32[256,128]{1,0:T(8,128)}, f32[2304,256]{1,0:T(8,128)}, f32[256,256]{1,0:T(8,128)}, f32[128,128]{1,0:T(8,128)}), (f32[256,128]{1,0:T(8,128)}, f32[2304,256]{1,0:T(8,128)}, f32[256,256]{1,0:T(8,128)}, ...) | async-done | bytes 2818064 | tf_op jit(solution)/shard_map/psum | solution.py:110
  674.6 1.3 fusion.46
  675.9 1.4 multiply_reduce_fusion.1
  677.3 1.5 multiply_reduce_fusion.2
  678.9 126.4 %all-reduce.1 = (f32[]{:T(128)}, f32[]{:T(128)}) all-reduce(f32[]{:T(128)} %get-tuple-element.48, f32[]{:T(128)} %multiply_reduce_fusion.1), channel_id=1, replica_groups=mesh['walker'=12,'orb'=64] {'orb'}, use_global_device_ids=true, to_apply=%region_7.8 | all-reduce | flops 2 | bytes 16 | tf_op jit(solution)/shard_map/psum | solution.py:126
  806.0 1.4 dynamic-slice_multiply_fusion
  808.7 1.5 multiply_add_fusion.4
  810.2 1.3 multiply_add_fusion.5
  (126 shorter events, 18.3 us)
Async XLA Ops:
  7.2 9.8 %copy-start = (bf16[2304,256]{1,0:T(8,128)(2,1)S(1)}, bf16[2304,256]{1,0:T(8,128)(2,1)}, u32[]{:S(2)}) copy-start(bf16[2304,256]{1,0:T(8,128)(2,1)} %param.12) | copy-start | bytes 3538948
  7.2 667.4 %all-reduce.4.cloned.1.call-start = ((), (), s32[]{:S(2)}) async-start(), calls=%async_computation | async-start | bytes 5636096 | tf_op jit(solution)/shard_map/psum | solution.py:110
  14.5 0.9 copy-start.1
  14.8 0.8 copy-start.2
  15.0 0.8 copy-start.3
  15.3 0.8 copy-start.5
  16.1 0.9 copy-start.6
  17.0 2.4 copy-start.22
  17.0 3.7 copy-start.18
  19.8 1.0 copy-start.8
  22.6 8.0 copy-start.19
  30.6 1.5 copy-start.17
  32.1 12.5 %copy-start.25 = (f32[4]{0:T(128)S(1)}, f32[4]{0:T(128)}, u32[]{:S(2)}) copy-start(f32[4]{0:T(128)} %param.10) | copy-start | bytes 52
  33.2 8.1 copy-start.4
  33.2 134.4 %copy-start.9 = (bf16[4,128,256]{2,1,0:T(8,128)(2,1)S(1)}, bf16[4,128,256]{2,1,0:T(8,128)(2,1)}, u32[]{:S(2)}) copy-start(bf16[4,128,256]{2,1,0:T(8,128)(2,1)} %copy-done.8) | copy-start | bytes 786436
  36.1 9.1 %copy-start.7 = (bf16[4,16,16,256]{3,2,1,0:T(8,128)(2,1)S(1)}, bf16[4,16,16,256]{3,2,1,0:T(8,128)(2,1)}, u32[]{:S(2)}) copy-start(bf16[4,16,16,256]{3,2,1,0:T(8,128)(2,1)} %copy-done.6) | copy-start | bytes 1572868
  41.3 128.3 %copy-start.10 = (f32[4,128,128]{2,1,0:T(8,128)S(1)}, f32[4,128,128]{2,1,0:T(8,128)}, u32[]{:S(2)}) copy-start(f32[4,128,128]{2,1,0:T(8,128)} %get-tuple-element.47) | copy-start | bytes 786436
  46.2 131.5 %copy-start.11 = (bf16[4,256,256]{1,2,0:T(8,128)(2,1)S(1)}, bf16[4,256,256]{1,2,0:T(8,128)(2,1)}, u32[]{:S(2)}) copy-start(bf16[4,256,256]{1,2,0:T(8,128)(2,1)} %copy.40) | copy-start | bytes 1572868
  167.5 6.9 copy-start.16
  167.5 7.7 copy-start.15
  167.5 8.6 %copy-start.14 = (bf16[4,256,256]{1,2,0:T(8,128)(2,1)S(1)}, bf16[4,256,256]{1,2,0:T(8,128)(2,1)}, u32[]{:S(2)}) copy-start(bf16[4,256,256]{1,2,0:T(8,128)(2,1)} %copy.38) | copy-start | bytes 1572868
  167.5 9.4 %copy-start.13 = (bf16[4,256,256]{1,2,0:T(8,128)(2,1)S(1)}, bf16[4,256,256]{1,2,0:T(8,128)(2,1)}, u32[]{:S(2)}) copy-start(bf16[4,256,256]{1,2,0:T(8,128)(2,1)} %copy.39) | copy-start | bytes 1572868
  170.8 8.7 %copy-start.12 = (bf16[4,256,256]{1,2,0:T(8,128)(2,1)S(1)}, bf16[4,256,256]{1,2,0:T(8,128)(2,1)}, u32[]{:S(2)}) copy-start(bf16[4,256,256]{1,2,0:T(8,128)(2,1)} %copy.42) | copy-start | bytes 1572868
  180.3 494.3 %copy-start.23 = (f32[4,256]{1,0:T(4,128)S(1)}, f32[4,256]{1,0:T(4,128)}, u32[]{:S(2)}) copy-start(f32[4,256]{1,0:T(4,128)} %param.16) | copy-start | bytes 12292
  180.3 497.0 %copy-start.21 = (f32[128,128]{1,0:T(8,128)S(1)}, f32[128,128]{1,0:T(8,128)}, u32[]{:S(2)}) copy-start(f32[128,128]{1,0:T(8,128)} %param.17) | copy-start | bytes 196612
  180.3 628.4 %copy-start.20 = (f32[128,128]{1,0:T(8,128)S(1)}, f32[128,128]{1,0:T(8,128)}, u32[]{:S(2)}) copy-start(f32[128,128]{1,0:T(8,128)} %param.15) | copy-start | bytes 196612
  180.3 629.9 %copy-start.24 = (f32[4,256]{1,0:T(4,128)S(1)}, f32[4,256]{1,0:T(4,128)}, u32[]{:S(2)}) copy-start(f32[4,256]{1,0:T(4,128)} %param.14) | copy-start | bytes 12292
Sparse Core Ops, SparseCore 0:
  185.8 488.7 all-reduce.3
where the time goes:
time: 819 us; the launch traced here: 818 us
  waiting for transfers between devices  489 us (60%)
  blocking collectives  247 us (30%)
  local copies, waits for them, and re-layouts  26.3 us (3%)
  matrix products  25.8 us (3%)
  between operations  16.7 us (2%)
  other arithmetic  13.5 us (2%)
    psum x1, waiting for transfers between devices, per_device(): lax.psum((input_gram, output_gram, head_part), ('walker', 'orb'))  489 us
    psum x1, blocking collectives, per_device(): head_norm, conv_norm = lax.psum((head_local, conv_local), 'orb')  126 us
    psum x1, blocking collectives, per_device(): energy_whole = lax.psum(energy_sum, ('walker', 'orb'))  121 us
  transfers between devices with their start and end apart: 1, of which 1 were waited for; matrix products, arithmetic and copies ran while one was open for 0% of the time, Pallas kernels for 0%

commit v1 on v0

v1 whole, which is shorter than its diff:
```python
import functools
import math

import jax
import jax.numpy as jnp
from jax import lax
from jax.experimental import pallas as pl
from jax.experimental.pallas import tpu as pltpu
from jax.sharding import PartitionSpec as P

L = 16
C = 256
NS_STEPS = 3
NE = 128
X_CHIPS = 4
TILES = 11

decay_rate = 0.8
MESH = pl.DeviceIdType.MESH


class Place:
    def __init__(self, nx, ny, nz):
        self.nx, self.ny, self.nz = nx, ny, nz
        self.z = lax.axis_index("walker")
        self.orb = lax.axis_index("orb")
        self.c = lax.rem(self.orb, 2)
        self.y = lax.rem(lax.div(self.orb, 2), ny)
        self.x = lax.div(self.orb, 2 * ny)
        self.k = self.x * 2 + self.c

    def at(self, x, y, c):
        return (self.z, (x * self.ny + y) * 2 + c)

    def core(self):
        return self.at(self.x, self.y, 1 - self.c)

    def along_x(self, d):
        return self.at(lax.rem(self.x + d, self.nx), self.y, self.c)

    def along_y(self, d):
        return self.at(self.x, lax.rem(self.y + d, self.ny), self.c)

    def along_k(self, d):
        k = lax.rem(self.k + d, 2 * self.nx)
        return self.at(lax.div(k, 2), self.y, lax.rem(k, 2))

    def along_z(self, d):
        return (lax.rem(self.z + d, self.nz), self.orb)

    def greet(self):
        barrier = pltpu.get_barrier_semaphore()
        peers = [self.along_y(d) for d in range(1, self.ny)]
        peers += [self.along_k(d) for d in range(1, 2 * self.nx)]
        peers += [self.along_z(d) for d in range(1, self.nz)]
        for peer in peers:
            pl.semaphore_signal(barrier, inc=1, device_id=peer, device_id_type=MESH)
        pl.semaphore_wait(barrier, len(peers))


class Sender:
    def __init__(self, send_sem, recv_sem):
        self.send_sem, self.recv_sem, self.used = send_sem, recv_sem, 0

    def __call__(self, source, target, device):
        copy = pltpu.make_async_remote_copy(
            src_ref=source,
            dst_ref=target,
            send_sem=self.send_sem.at[self.used],
            recv_sem=self.recv_sem.at[self.used],
            device_id=device,
            device_id_type=MESH,
        )
        copy.start()
        self.used += 1
        return copy


def wait_all(copies):
    for copy in copies:
        copy.wait()


def total_of(first, ref, count):
    total = first
    for i in range(count):
        total = total + ref[i]
    return total


def spread(place, slots_ref, out_ref):
    for i in range(2 * place.nx):
        k = lax.rem(place.k - i + 2 * place.nx, 2 * place.nx)
        for j in range(place.ny):
            y = lax.rem(place.y - j + place.ny, place.ny)
            out_ref[k, y] = slots_ref[i, j]


def gather_kernel(
    nx, ny, nz, rows_ref, energy_ref, gathered_ref, total_ref,
    rows_y, rows_k, energy_y, energy_k, energy_z, part_k, part_z, send_sem, recv_sem,
):
    place = Place(nx, ny, nz)
    place.greet()
    send = Sender(send_sem, recv_sem)
    energies = [send(energy_ref, energy_y.at[d - 1], place.along_y(d)) for d in range(1, ny)]
    rows = [send(rows_ref, rows_y.at[d], place.along_y(d)) for d in range(1, ny)]
    rows_y[0] = rows_ref[...]
    wait_all(energies)
    part_k[...] = total_of(energy_ref[...], energy_y, ny - 1)
    energies = [send(part_k, energy_k.at[d - 1], place.along_k(d)) for d in range(1, 2 * nx)]
    wait_all(rows)
    rows = [send(rows_y, rows_k.at[d], place.along_k(d)) for d in range(1, 2 * nx)]
    rows_k[0] = rows_y[...]
    wait_all(energies)
    part_z[...] = total_of(part_k[...], energy_k, 2 * nx - 1)
    energies = [send(part_z, energy_z.at[d - 1], place.along_z(d)) for d in range(1, nz)]
    wait_all(rows)
    spread(place, rows_k, gathered_ref)
    wait_all(energies)
    total_ref[...] = total_of(part_z[...], energy_z, nz - 1)


def gather(nx, ny, nz, rows, energy):
    tile = (8, 128)
    copies = 2 * (ny - 1) + 2 * (2 * nx - 1) + nz - 1
    return pl.pallas_call(
        functools.partial(gather_kernel, nx, ny, nz),
        name="gather_rows",
        out_shape=(
            jax.ShapeDtypeStruct((2 * nx, ny) + tile, jnp.float32),
            jax.ShapeDtypeStruct(tile, jnp.float32),
        ),
        in_specs=[pl.BlockSpec(memory_space=pltpu.VMEM)] * 2,
        out_specs=[pl.BlockSpec(memory_space=pltpu.VMEM)] * 2,
        scratch_shapes=[
            pltpu.VMEM((ny,) + tile, jnp.float32),
            pltpu.VMEM((2 * nx, ny) + tile, jnp.float32),
            pltpu.VMEM((ny - 1,) + tile, jnp.float32),
            pltpu.VMEM((2 * nx - 1,) + tile, jnp.float32),
            pltpu.VMEM((nz - 1,) + tile, jnp.float32),
            pltpu.VMEM(tile, jnp.float32),
            pltpu.VMEM(tile, jnp.float32),
            pltpu.SemaphoreType.DMA((copies,)),
            pltpu.SemaphoreType.DMA((copies,)),
        ],
        compiler_params=pltpu.CompilerParams(collective_id=0, has_side_effects=True),
    )(rows, energy)


def reduce_kernel(
    nx, ny, nz, parts_ref, chunk_ref, gathered_ref,
    from_core, sum_core, from_x, sum_x, from_y, sum_y, from_z, sum_z, got_z,
    block, block_y, block_k, send_sem, recv_sem,
):
    place = Place(nx, ny, nz)
    place.greet()
    send = Sender(send_sem, recv_sem)
    order = [*range(1, nx), 0]
    other = 1 - place.c
    at_x = [lax.rem(place.x + d, nx) for d in order]
    copies = [send(parts_ref.at[other, i], from_core.at[i], place.core()) for i in at_x]
    sent = []
    for d, i, copy in zip(order, at_x, copies):
        copy.wait()
        sum_core[i] = parts_ref[place.c, i] + from_core[i]
        if d:
            sent.append(send(sum_core.at[i], from_x.at[d - 1], place.along_x(d)))
    wait_all(sent)
    sum_x[...] = total_of(sum_core[place.x], from_x, nx - 1)
    wait_all(
        [
            send(sum_x.at[lax.rem(place.y + d, ny)], from_y.at[d - 1], place.along_y(d))
            for d in range(1, ny)
        ]
    )
    sum_y[...] = jnp.zeros_like(sum_y)
    sum_y[0:TILES] = total_of(sum_x[place.y], from_y, ny - 1)
    wait_all(
        [
            send(sum_y.at[lax.rem(place.z + d, nz)], from_z.at[d - 1], place.along_z(d))
            for d in range(1, nz)
        ]
    )
    sum_z[...] = total_of(sum_y[place.z], from_z, nz - 1)
    copies = [send(sum_z, got_z.at[d], place.along_z(d)) for d in range(1, nz)]
    chunk_ref[place.z] = sum_z[...]
    wait_all(copies)
    for d in range(1, nz):
        chunk_ref[lax.rem(place.z - d + nz, nz)] = got_z[d]
    conv = chunk_ref[0:9]
    squares = jnp.sum(jnp.sum(conv * conv, axis=0), axis=0, keepdims=True)
    row = lax.broadcasted_iota(jnp.int32, (8, 128), 0)
    block[...] = jnp.where(row == 6, jnp.broadcast_to(squares, (8, 128)), chunk_ref[TILES - 1])
    copies = [send(block, block_y.at[d], place.along_y(d)) for d in range(1, ny)]
    block_y[0] = block[...]
    wait_all(copies)
    copies = [send(block_y, block_k.at[d], place.along_k(d)) for d in range(1, 2 * nx)]
    block_k[0] = block_y[...]
    wait_all(copies)
    spread(place, block_k, gathered_ref)


def reduce(nx, ny, nz, parts):
    tile = (8, 128)
    copies = nx + (nx - 1) + 2 * (ny - 1) + 2 * (nz - 1) + 2 * nx - 1

    def buffer(*lead):
        return pltpu.VMEM(lead + tile, jnp.float32)

    return pl.pallas_call(
        functools.partial(reduce_kernel, nx, ny, nz),
        name="reduce_parts",
        out_shape=(
            jax.ShapeDtypeStruct((nz,) + tile, jnp.float32),
            jax.ShapeDtypeStruct((2 * nx, ny) + tile, jnp.float32),
        ),
        in_specs=[pl.BlockSpec(memory_space=pltpu.VMEM)],
        out_specs=[pl.BlockSpec(memory_space=pltpu.VMEM)] * 2,
        scratch_shapes=[
            buffer(nx, ny, TILES),
            buffer(nx, ny, TILES),
            buffer(nx - 1, ny, TILES),
            buffer(ny, TILES),
            buffer(ny - 1, TILES),
            buffer(nz),
            buffer(nz - 1),
            buffer(),
            buffer(nz),
            buffer(),
            buffer(ny),
            buffer(2 * nx, ny),
            pltpu.SemaphoreType.DMA((copies,)),
            pltpu.SemaphoreType.DMA((copies,)),
        ],
        compiler_params=pltpu.CompilerParams(collective_id=1, has_side_effects=True),
    )(parts)


def by_place(nx, ny, array, width):
    rows = array.shape[0] // (2 * nx * ny)
    split = array.reshape(nx, ny, 2, rows, width // 128, 128)
    return split.transpose(2, 0, 1, 4, 3, 5).reshape(2, nx, ny, rows * width // 128, 128)


def in_order(nx, ny, gathered):
    split = gathered.reshape(nx, 2, ny, gathered.shape[-2], 128)
    return split.transpose(0, 2, 1, 3, 4).reshape(2 * nx * ny, gathered.shape[-2], 128)


def widen(rows):
    half = rows.shape[-2] // 2
    return jnp.concatenate([rows[..., :half, :], rows[..., half:, :]], axis=-1)


def neighbours(lattice):
    shifted_views = [
        jnp.roll(lattice, (-shift_x, -shift_y), axis=(1, 2))
        for shift_x in (-1, 0, 1)
        for shift_y in (-1, 0, 1)
    ]
    return jnp.concatenate(shifted_views, axis=-1)


def local_parts(occupations, weights, embed_weight, conv_weight, head_weight):
    sample_count = occupations.shape[0]
    site_count = L * L
    site_ids = jnp.arange(site_count, dtype=jnp.int32)
    select = (occupations[:, :, None] == site_ids[None, None, :]).astype(jnp.bfloat16)
    half_count = NE // 2
    up_fill = jnp.sum(select[:, :half_count].astype(jnp.float32), axis=1)
    down_fill = jnp.sum(select[:, half_count:].astype(jnp.float32), axis=1)
    lattice = (
        jnp.stack([up_fill, down_fill], axis=-1).reshape(sample_count, L, L, 2).astype(jnp.bfloat16)
    )
    embed_in = neighbours(lattice).reshape(sample_count * site_count, 18)
    embedded = jnp.tanh(jnp.dot(embed_in, embed_weight, preferred_element_type=jnp.float32)).astype(
        jnp.bfloat16
    )
    patches = neighbours(embedded.reshape(sample_count, L, L, C)).reshape(
        sample_count * site_count, 9 * C
    )
    conv_pre = jnp.dot(patches, conv_weight, preferred_element_type=jnp.float32)
    squash = jnp.tanh(conv_pre)
    hidden = (
        (embedded.astype(jnp.float32) + squash)
        .astype(jnp.bfloat16)
        .reshape(sample_count, site_count, C)
    )
    electron_rows = jnp.einsum(
        "bis,bsc->bic", select, hidden, preferred_element_type=jnp.float32
    ).astype(jnp.bfloat16)
    flat_rows = electron_rows.reshape(sample_count * NE, C)
    logits = jnp.dot(flat_rows, head_weight, preferred_element_type=jnp.float32).reshape(
        sample_count, NE, NE
    )
    orbital_tanh = jnp.tanh(logits)
    identity = jnp.eye(NE, dtype=jnp.float32)
    slater_scale = 0.35 / math.sqrt(NE)
    slater = identity + slater_scale * orbital_tanh
    inverse_est = 2.0 * identity - slater
    for sweep in range(NS_STEPS - 1):
        product = jnp.einsum("bij,bjk->bik", slater, inverse_est, precision=lax.Precision.HIGHEST)
        inverse_est = jnp.einsum(
            "bij,bjk->bik", inverse_est, 2.0 * identity - product, precision=lax.Precision.HIGHEST
        )
    log_grads = (1.0 - orbital_tanh * orbital_tanh) * jnp.swapaxes(inverse_est, 1, 2)
    cotangent = (slater_scale * log_grads).astype(jnp.bfloat16)
    weighted = (weights[:, None, None] * (slater_scale * log_grads)).astype(jnp.bfloat16)
    head_part = jnp.dot(
        flat_rows.T, weighted.reshape(sample_count * NE, NE), preferred_element_type=jnp.float32
    )
    input_gram = jnp.einsum("nc,nd->cd", flat_rows, flat_rows, preferred_element_type=jnp.float32)
    flat_grads = log_grads.reshape(sample_count * NE, NE)
    output_gram = jnp.dot(flat_grads.T, flat_grads, precision=lax.Precision.HIGHEST)
    row_grads = (
        jnp.dot(
            cotangent.reshape(sample_count * NE, NE),
            head_weight.T,
            preferred_element_type=jnp.float32,
        )
        .astype(jnp.bfloat16)
        .reshape(sample_count, NE, C)
    )
    hidden_grad = jnp.einsum("bis,bic->bsc", select, row_grads, preferred_element_type=jnp.float32)
    pre_grad = (
        (weights[:, None, None] * hidden_grad).reshape(sample_count * site_count, C)
        * (1.0 - squash * squash)
    ).astype(jnp.bfloat16)
    conv_part = jnp.dot(patches.T, pre_grad, preferred_element_type=jnp.float32)
    return conv_part, input_gram, head_part, output_gram


def per_device(
    nx,
    ny,
    nz,
    occupations,
    local_energy,
    embed_weight,
    conv_weight,
    head_weight,
    a_factor,
    g_factor,
    a_inverse,
    g_inverse,
):
    samples_all = occupations.shape[0] * 2 * nx * ny * nz
    inverse_tile = jnp.concatenate([a_inverse[:, :128], a_inverse[:, 128:]], axis=0)
    energy_tile = jnp.broadcast_to(jnp.sum(local_energy), (8, 128))
    inverse_tiles, energy_whole = gather(nx, ny, nz, inverse_tile, energy_tile)
    mean_energy = energy_whole[0, 0] / samples_all
    weights = (local_energy - mean_energy) / samples_all
    conv_part, input_gram, head_part, output_gram = local_parts(
        occupations, weights, embed_weight, conv_weight, head_weight
    )
    output_rows = by_place(nx, ny, output_gram, NE)
    parts = jnp.concatenate(
        [
            by_place(nx, ny, conv_part, C),
            by_place(nx, ny, input_gram, C),
            by_place(nx, ny, head_part, NE),
            jnp.pad(output_rows, ((0, 0),) * 3 + ((0, 4 - output_rows.shape[3]), (0, 0))),
        ],
        axis=3,
    ).reshape(2, nx, ny, TILES, 8, 128)
    chunk, gathered = reduce(nx, ny, nz, parts)
    chunk = chunk.reshape(nz * 8, 128)
    conv_panel = widen(chunk[:72])
    input_rows = widen(chunk[72:80])
    blocks = in_order(nx, ny, gathered)
    head_grad = blocks[:, 0:4].reshape(C, NE)
    output_sum = blocks[:, 4:6].reshape(NE, NE)
    conv_norm = jnp.sum(blocks[:, 6])
    inverse_whole = widen(in_order(nx, ny, inverse_tiles)).reshape(C, C)
    left_applied = jnp.dot(inverse_whole, head_grad, precision=lax.Precision.HIGHEST)
    precond = jnp.dot(left_applied, g_inverse, precision=lax.Precision.HIGHEST)
    head_norm = jnp.sum(precond * head_grad)
    head_rows = C // (2 * nx * ny)
    precond_rows = lax.dynamic_slice_in_dim(
        precond, lax.axis_index("orb") * head_rows, head_rows, 0
    )
    head_update = -jnp.sqrt(C * NE / 4.0 / head_norm) * precond_rows
    conv_update = -jnp.sqrt(9 * C * C / 4.0 / conv_norm) * conv_panel
    new_a_factor = decay_rate * a_factor + (1.0 - decay_rate) * input_rows / (samples_all * NE)
    new_g_factor = decay_rate * g_factor + (1.0 - decay_rate) * output_sum / samples_all
    return (head_update, conv_update, new_a_factor, new_g_factor)


def solution(mesh):
    nz, orb = mesh.shape["walker"], mesh.shape["orb"]
    in_specs = (
        P(("walker", "orb"), None),
        P(("walker", "orb")),
        P(),
        P(),
        P(),
        P("orb", None),
        P(),
        P("orb", None),
        P(),
    )
    out_specs = (P("orb", None), P("orb", None), P("orb", None), P())
    return jax.shard_map(
        functools.partial(per_device, X_CHIPS, orb // (2 * X_CHIPS), nz),
        mesh=mesh,
        in_specs=in_specs,
        out_specs=out_specs,
        check_vma=False,
    )
```

time: 819 us -> 156 us (0.19)
  waiting for transfers between devices: 489 us -> 0 us
  blocking collectives: 247 us -> 0 us
  Pallas kernels: 0 us -> 98.2 us
  between operations: 16.7 us -> 3.39 us
  matrix products: 25.8 us -> 13.8 us
    psum x1 -> x0, waiting for transfers between devices: 489 us -> none  [per_device(): lax.psum((input_gram, output_gram, head_part), ('walker', 'orb'))]
    psum x2 -> x0, blocking collectives: 247 us -> none  [the longest x1 126 us: per_device(): head_norm, conv_norm = lax.psum((head_local, conv_local), 'orb')]
    pallas_call x0 -> x2, Pallas kernels: none -> 98.2 us  [the longest x1 61.9 us: reduce(): pl.pallas_call(functools.partial(reduce_kernel, nx, ny, nz), name='reduce...]
    dot_general x0 -> x5, local copies, waits for them, and re-layouts: none -> 16.1 us  [the longest x3 14.2 us: local_parts(): conv_part = jnp.dot(patches.T, pre_grad, preferred_element_type=jnp.float32)]
    concatenate x20 -> x10, local copies, waits for them, and re-layouts: 13.3 us -> 0.95 us  [neighbours(): return jnp.concatenate(shifted_views, axis=-1)]
    dot_general x18 -> x16, matrix products: 25.8 us -> 13.8 us  [the longest x1 3.76 us: local_parts(): conv_part = jnp.dot(patches.T, pre_grad, preferred_element_type=jnp.float32)]
    unnamed x71 -> x37, local copies, waits for them, and re-layouts: 10.6 us -> 1.05 us
  transfers between devices with their start and end apart: 1 -> 0, of which waited for: 1 -> 0; matrix products, arithmetic and copies ran while one was open for 0% -> 0% of each run, Pallas kernels for 0% -> 0%
where the time goes in v1:
time: 156 us; the launch traced here: 155 us
  Pallas kernels  98.2 us (63%)
  local copies, waits for them, and re-layouts  30.1 us (19%)
  matrix products  13.8 us (9%)
  other arithmetic  9.52 us (6%)
  between operations  3.39 us (2%)
    pallas_call x1, Pallas kernels, reduce(): pl.pallas_call(functools.partial(reduce_kernel, nx, ny, nz), name='reduce...  61.9 us
    pallas_call x1, Pallas kernels, gather(): pl.pallas_call(functools.partial(gather_kernel, nx, ny, nz), name='gather...  36.3 us
    dot_general x3, local copies, waits for them, and re-layouts, local_parts(): conv_part = jnp.dot(patches.T, pre_grad, preferred_element_type=jnp.float32)  14.2 us
    dot_general x1, matrix products, local_parts(): conv_part = jnp.dot(patches.T, pre_grad, preferred_element_type=jnp.float32)  3.76 us

profile of v1, /device:TPU:1, one launch (start us, length us, event | category | flops | bytes accessed | tf_op | source)
XLA Modules:
  0.0 155.0 jit_solution(6062080903112847548)
XLA Ops:
  0.6 0.8 fusion.11
  3.9 1.0 fusion.5
  7.8 1.4 add_convert_fusion
  9.2 0.7 copy-done.1
  10.8 0.7 copy.29
  11.5 0.6 pad_maximum_fusion.17.rows_ref
  12.1 0.6 reduce_sum.45
  12.7 1.2 broadcast_in_dim.2.energy_ref
  14.0 36.3 %gather_rows.1 = (f32[8,8,8,128]{3,2,1,0:T(8,128)}, f32[8,128]{1,0:T(8,128)}) custom-call(f32[8,128]{1,0:T(8,128)} %pad_maximum_fusion.17.rows_ref, f32[8,128]{1,0:T(8,128)} %broadcast_in_dim.2.energy_ref), custom_call_target="tpu_custom_call" | custom-call | tf_op jit(solution)/shard_map/gather_rows/pallas_call | solution.py:127
  50.3 1.2 slice.256
  52.8 0.4 fusion.12
  53.7 1.4 multiply_convert_fusion.1
  56.0 6.8 %copy.22 = bf16[2304,1024]{1,0:T(8,128)(2,1)} copy(bf16[2304,1024]{0,1:T(8,128)(2,1)} %bitcast.156) | data formatting | bytes 9437184 | tf_op jit(solution)/shard_map/dot_general | solution.py:330
  62.8 7.2 %reshape.165 = bf16[4,8,2,36,1024,1]{4,3,2,1,0,5:T(8,128)(2,1)} reshape(bf16[2304,1024]{1,0:T(8,128)(2,1)} %copy.22) | data formatting | bytes 9437184 | tf_op jit(solution)/shard_map/dot_general | solution.py:330
  70.0 3.8 %fusion.2 = f32[2,4,8,2,36,128]{5,4,3,0,2,1:T(8,128)S(1)} fusion(bf16[2,128,1024,1,1,1]{2,1,0,5,4,3:T(8,128)(2,1)S(1)} %bitcast.183, bf16[4,8,2,36,1024,1]{4,3,2,1,0,5:T(8,128)(2,1)} %reshape.165), kind=kOutput, calls=%fused_computation.5 | convolution fusion | flops 1207959552 | bytes 7602176 | tf_op jit(solution)/shard_map/dot_general | solution.py:330
  73.7 1.4 copy.26
  75.1 0.9 convolution_bitcast_fusion.1
  76.0 1.8 %copy.31 = f32[512,128]{0,1:T(8,128)} copy(f32[512,128]{1,0:T(8,128)} %bitcast.159) | data formatting | bytes 524288 | tf_op jit(solution)/shard_map/reshape | solution.py:314
  77.8 1.8 %dot_general.92 = f32[4,8,2,2,512]{4,3,2,1,0:T(2,128)} reshape(f32[128,512]{1,0:T(8,128)} %bitcast.177) | data formatting | bytes 524288 | tf_op jit(solution)/shard_map/dot_general | solution.py:315
  79.6 1.5 convolution_bitcast_fusion.2
  81.1 1.2 select_maximum_fusion
  82.3 2.1 %copy.62 = f32[2,4,8,88,128]{4,3,2,1,0:T(8,128)} copy(f32[2,4,8,88,128]{4,2,3,1,0:T(8,128)S(1)} %select_maximum_fusion) | data formatting | bytes 5767168 | tf_op jit(solution)/shard_map/concatenate | solution.py:358
  84.4 61.9 %reduce_parts.1 = (f32[12,8,128]{2,1,0:T(8,128)}, f32[8,8,8,128]{3,2,1,0:T(8,128)}) custom-call(f32[2,4,8,11,8,128]{5,4,3,2,1,0:T(8,128)} %bitcast.154), custom_call_target="tpu_custom_call" | custom-call | tf_op jit(solution)/shard_map/reduce_parts/pallas_call | solution.py:211
  146.3 1.0 copy.36
  148.0 0.9 multiply_reduce_fusion
  149.6 0.6 dynamic-slice_multiply_fusion
  150.2 0.8 slice_bitcast_fusion
  150.9 0.7 slice_reduce_fusion.2
  152.3 0.6 maximum_multiply_fusion
  153.0 0.7 slice_bitcast_fusion.2
  153.7 0.6 fusion.43
  154.4 0.6 multiply_add_fusion.4
  (101 shorter events, 8.4 us)
Async XLA Ops:
  0.6 7.1 %copy-start = (bf16[2304,256]{1,0:T(8,128)(2,1)S(1)}, bf16[2304,256]{1,0:T(8,128)(2,1)}, u32[]{:S(2)}) copy-start(bf16[2304,256]{1,0:T(8,128)(2,1)} %param.12) | copy-start | bytes 3538948
  7.8 2.1 %copy-start.1 = (bf16[1024,2304]{1,0:T(8,128)(2,1)}, bf16[1024,2304]{1,0:T(8,128)(2,1)S(1)}, u32[]{:S(2)}) copy-start(bf16[1024,2304]{1,0:T(8,128)(2,1)S(1)} %constant_dynamic-update-slice_fusion.2) | copy-start | bytes 14155780
  7.8 2.1 %copy-start.9 = (s32[4,128]{1,0:T(4,128)S(1)}, s32[4,128]{1,0:T(4,128)}, u32[]{:S(2)}) copy-start(s32[4,128]{1,0:T(4,128)} %param.9) | copy-start | bytes 6148
  7.8 3.7 %copy-start.11 = (f32[4,256]{1,0:T(4,128)S(1)}, f32[4,256]{1,0:T(4,128)}, u32[]{:S(2)}) copy-start(f32[4,256]{1,0:T(4,128)} %param.16) | copy-start | bytes 12292
  7.8 4.3 %copy-start.12 = (f32[4]{0:T(128)S(1)}, f32[4]{0:T(128)}, u32[]{:S(2)}) copy-start(f32[4]{0:T(128)} %param.10) | copy-start | bytes 52
  7.8 44.3 %copy-start.5 = (bf16[256,128]{1,0:T(8,128)(2,1)S(1)}, bf16[256,128]{1,0:T(8,128)(2,1)}, u32[]{:S(2)}) copy-start(bf16[256,128]{1,0:T(8,128)(2,1)} %param.13) | copy-start | bytes 196612
  10.5 45.2 %copy-start.2 = (bf16[4,8,2,4,512]{4,3,2,1,0:T(4,128)(2,1)}, bf16[4,8,2,4,512]{4,3,2,1,0:T(4,128)(2,1)S(1)}, u32[]{:S(2)}) copy-start(bf16[4,8,2,4,512]{4,3,2,1,0:T(4,128)(2,1)S(1)} %dot_general.86) | copy-start | bytes 786436
  70.0 5.2 %copy-start.3 = (bf16[4,8,2,4,512]{4,3,2,1,0:T(4,128)(2,1)S(1)}, bf16[4,8,2,4,512]{4,3,2,1,0:T(4,128)(2,1)}, u32[]{:S(2)}) copy-start(bf16[4,8,2,4,512]{4,3,2,1,0:T(4,128)(2,1)} %copy-done.2) | copy-start | bytes 786436
  70.0 5.2 %copy-start.4 = (bf16[4,128,128]{2,1,0:T(8,128)(2,1)S(1)}, bf16[4,128,128]{2,1,0:T(8,128)(2,1)}, u32[]{:S(2)}) copy-start(bf16[4,128,128]{2,1,0:T(8,128)(2,1)} %get-tuple-element.31) | copy-start | bytes 393220
  82.3 65.0 %copy-start.6 = (f32[8,8,8,128]{3,2,1,0:T(8,128)S(1)}, f32[8,8,8,128]{3,2,1,0:T(8,128)}, u32[]{:S(2)}) copy-start(f32[8,8,8,128]{3,2,1,0:T(8,128)} %get-tuple-element.8) | copy-start | bytes 786436
  82.3 65.7 %copy-start.8 = (f32[128,128]{1,0:T(8,128)S(1)}, f32[128,128]{1,0:T(8,128)}, u32[]{:S(2)}) copy-start(f32[128,128]{1,0:T(8,128)} %param.17) | copy-start | bytes 196612
  84.4 69.3 %copy-start.10 = (f32[4,256]{1,0:T(4,128)S(1)}, f32[4,256]{1,0:T(4,128)}, u32[]{:S(2)}) copy-start(f32[4,256]{1,0:T(4,128)} %param.14) | copy-start | bytes 12292
  84.4 70.0 %copy-start.7 = (f32[128,128]{1,0:T(8,128)S(1)}, f32[128,128]{1,0:T(8,128)}, u32[]{:S(2)}) copy-start(f32[128,128]{1,0:T(8,128)} %param.15) | copy-start | bytes 196612

commit v2 on v1

--- a/solution.py
+++ b/solution.py
@@ -48,14 +48,17 @@
     def along_z(self, d):
         return (lax.rem(self.z + d, self.nz), self.orb)
 
-    def greet(self):
+    def signal_peers(self):
         barrier = pltpu.get_barrier_semaphore()
         peers = [self.along_y(d) for d in range(1, self.ny)]
         peers += [self.along_k(d) for d in range(1, 2 * self.nx)]
         peers += [self.along_z(d) for d in range(1, self.nz)]
         for peer in peers:
             pl.semaphore_signal(barrier, inc=1, device_id=peer, device_id_type=MESH)
-        pl.semaphore_wait(barrier, len(peers))
+        return len(peers)
+
+    def wait_peers(self, count):
+        pl.semaphore_wait(pltpu.get_barrier_semaphore(), count)
 
 
 class Sender:
@@ -96,56 +99,246 @@
             out_ref[k, y] = slots_ref[i, j]
 
 
-def gather_kernel(
-    nx, ny, nz, rows_ref, energy_ref, gathered_ref, total_ref,
-    rows_y, rows_k, energy_y, energy_k, energy_z, part_k, part_z, send_sem, recv_sem,
+def site_shift_y(field, b):
+    if b == 0:
+        return field
+    y = lax.broadcasted_iota(jnp.int32, field.shape, 0) & (L - 1)
+    sites = field.shape[0]
+    if b == 1:
+        edge, inside = pltpu.roll(field, L - 1, 0), pltpu.roll(field, sites - 1, 0)
+        return jnp.where(y == L - 1, edge, inside)
+    edge, inside = pltpu.roll(field, sites - L + 1, 0), pltpu.roll(field, 1, 0)
+    return jnp.where(y == 0, edge, inside)
+
+
+def site_shift_x(field, a):
+    if a == 0:
+        return field
+    cut = L if a == 1 else field.shape[0] - L
+    return jnp.concatenate([field[cut:], field[:cut]], axis=0)
+
+
+def site_patches(field, sign):
+    by_y = {b: site_shift_y(field, sign * b).astype(jnp.bfloat16) for b in (-1, 0, 1)}
+    return jnp.concatenate(
+        [site_shift_x(by_y[b], sign * a) for a in (-1, 0, 1) for b in (-1, 0, 1)], axis=1
+    )
+
+
+def multiply(left, right):
+    return jnp.dot(
+        left.astype(jnp.bfloat16), right.astype(jnp.bfloat16), preferred_element_type=jnp.float32
+    )
+
+
+def electrons_by_site(occ_ref, b):
+    sites = lax.broadcasted_iota(jnp.int32, (L * L, NE), 0)
+    return (sites == occ_ref[b]).astype(jnp.float32).astype(jnp.bfloat16)
+
+
+def forward(b, occ_ref, occ_t_ref, embed_ref, conv_w_ref, head_w_ref,
+            embedded_ref, slope_ref, rows_ref, log_ref):
+    by_site = electrons_by_site(occ_ref, b)
+    electron = lax.broadcasted_iota(jnp.int32, (NE, 128), 0)
+    lane = lax.broadcasted_iota(jnp.int32, (NE, 128), 1)
+    down = (electron >= NE // 2).astype(jnp.int32)
+    spin = ((lane & 1) == down).astype(jnp.float32)
+    counts = multiply(by_site, spin)
+    tap_of_lane = lax.broadcasted_iota(jnp.int32, counts.shape, 1) >> 1
+    near = jnp.zeros_like(counts)
+    for j in (-1, 0, 1):
+        at_y = site_shift_y(counts, j)
+        for i in (-1, 0, 1):
+            tap = (i + 1) * 3 + j + 1
+            near = jnp.where(tap_of_lane == tap, site_shift_x(at_y, i), near)
+    embedded = jnp.tanh(multiply(near, embed_ref[...])).astype(jnp.bfloat16)
+    embedded_ref[b] = embedded
+    wide = embedded.astype(jnp.float32)
+    squash = jnp.tanh(multiply(site_patches(wide, 1), conv_w_ref[...]))
+    slope_ref[b] = 1.0 - squash * squash
+    hidden = (wide + squash).astype(jnp.bfloat16)
+    sites = lax.broadcasted_iota(jnp.int32, (NE, L * L), 1)
+    select = (occ_t_ref[b] == sites).astype(jnp.float32)
+    rows = multiply(select, hidden).astype(jnp.bfloat16)
+    rows_ref[b] = rows
+    orbital_tanh = jnp.tanh(multiply(rows, head_w_ref[...]))
+    shift = (0.35 / math.sqrt(NE)) * orbital_tanh
+    row = lax.broadcasted_iota(jnp.int32, (NE, NE), 0)
+    column = lax.broadcasted_iota(jnp.int32, (NE, NE), 1)
+    identity = (row == column).astype(jnp.float32)
+    second = multiply(shift, shift)
+    inverse_est = identity - shift + second - multiply(shift, second)
+    inverse_est = inverse_est + multiply(inverse_est, multiply(second, second))
+    log_ref[b] = (1.0 - orbital_tanh * orbital_tanh) * inverse_est.T
+
+
+def backward(b, occ_ref, head_w_ref, slope_ref, log_ref, cot_ref, pre_ref):
+    cotangent = ((0.35 / math.sqrt(NE)) * log_ref[b]).astype(jnp.bfloat16)
+    cot_ref[b] = cotangent
+    row_grads = lax.dot_general(
+        cotangent, head_w_ref[...], (((1,), (1,)), ((), ())), preferred_element_type=jnp.float32
+    ).astype(jnp.bfloat16)
+    hidden_grad = multiply(electrons_by_site(occ_ref, b), row_grads)
+    pre_ref[b] = (hidden_grad * slope_ref[b]).astype(jnp.bfloat16)
+
+
+def grams(samples, rows_ref, log_ref, rows_t_ref, input_ref, output_ref):
+    rows = rows_ref[...].reshape(samples * NE, C)
+    rows_t = rows.astype(jnp.float32).T.astype(jnp.bfloat16)
+    rows_t_ref[...] = rows_t
+    input_ref[...] = multiply(rows_t, rows)
+    logs = log_ref[...].reshape(samples * NE, NE)
+    output_ref[...] = jnp.dot(
+        logs.T, logs, precision=lax.Precision.HIGHEST, preferred_element_type=jnp.float32
+    )
+
+
+def weighted_sums(samples, weight_of, embedded_ref, pre_ref, rows_t_ref, cot_ref, conv_ref, head_ref):
+    for b in range(samples):
+        weight = weight_of(b)
+        wide = jnp.concatenate([weight, weight], axis=1)
+        embedded_t = embedded_ref[b].astype(jnp.float32).T
+        terms = multiply(embedded_t, site_patches(pre_ref[b].astype(jnp.float32), -1))
+        head = weight * multiply(rows_t_ref[:, b * NE : (b + 1) * NE], cot_ref[b])
+        head_ref[...] = head if b == 0 else head_ref[...] + head
+        for tap in range(9):
+            rows = slice(tap * C, (tap + 1) * C)
+            term = wide * terms[:, rows]
+            conv_ref[rows, :] = term if b == 0 else conv_ref[rows, :] + term
+
+
+def lay_out(nx, ny, conv_ref, input_ref, head_ref, output_ref, parts_ref):
+    row = lax.broadcasted_iota(jnp.int32, (8, 128), 0)
+
+    def halves(first, second, c):
+        if c == 0:
+            return jnp.where(row < 4, first, pltpu.roll(second, 4, 0))
+        return jnp.where(row < 4, pltpu.roll(first, 4, 0), second)
+
+    for pair in range(nx * ny):
+        x, y = pair // ny, pair % ny
+        for c in range(2):
+            top = 72 * pair + 40 * c
+            for half in range(2):
+                lanes = slice(128 * half, 128 * half + 128)
+                for i in range(4):
+                    tile = conv_ref[top + 8 * i : top + 8 * i + 8, lanes]
+                    parts_ref[c, x, y, 4 * half + i] = tile
+            middle = slice(72 * pair + 32, 72 * pair + 40)
+            parts_ref[c, x, y, 8] = halves(conv_ref[middle, :128], conv_ref[middle, 128:], c)
+            eight = slice(8 * pair, 8 * pair + 8)
+            parts_ref[c, x, y, 9] = halves(input_ref[eight, :128], input_ref[eight, 128:], c)
+            place = 4 * (pair % 2) + 2 * c
+            output = output_ref[8 * (pair // 2) : 8 * (pair // 2) + 8, :]
+            output = pltpu.roll(output, (4 - place) % 8, 0) if place != 4 else output
+            head = head_ref[eight, :] if c == 0 else pltpu.roll(head_ref[eight, :], 4, 0)
+            parts_ref[c, x, y, 10] = jnp.where(row < 4, head, output)
+
+
+def parts_kernel(
+    nx, ny, nz, samples,
+    occ_ref, occ_t_ref, energy_ref, inverse_ref, embed_ref, conv_w_ref, head_w_ref,
+    parts_ref, gathered_ref,
+    rows_y, rows_k, energy_own, energy_y, energy_k, energy_z, part_k, part_z,
+    embedded_ref, slope_ref, rows_ref, log_ref, cot_ref, pre_ref, rows_t_ref,
+    input_ref, output_ref, conv_ref, head_ref, send_sem, recv_sem,
 ):
     place = Place(nx, ny, nz)
-    place.greet()
+    energy_own[...] = total_of(energy_ref[0], energy_ref.at[1:], samples - 1)
+    peers = place.signal_peers()
+
+    def sample(b):
+        forward(b, occ_ref, occ_t_ref, embed_ref, conv_w_ref, head_w_ref,
+                embedded_ref, slope_ref, rows_ref, log_ref)
+
     send = Sender(send_sem, recv_sem)
-    energies = [send(energy_ref, energy_y.at[d - 1], place.along_y(d)) for d in range(1, ny)]
-    rows = [send(rows_ref, rows_y.at[d], place.along_y(d)) for d in range(1, ny)]
-    rows_y[0] = rows_ref[...]
+    sample(0)
+    place.wait_peers(peers)
+    energies = [send(energy_own, energy_y.at[d - 1], place.along_y(d)) for d in range(1, ny)]
+    rows = [send(inverse_ref, rows_y.at[d], place.along_y(d)) for d in range(1, ny)]
+    rows_y[0] = inverse_ref[...]
+    sample(1)
     wait_all(energies)
-    part_k[...] = total_of(energy_ref[...], energy_y, ny - 1)
+    part_k[...] = total_of(energy_own[...], energy_y, ny - 1)
     energies = [send(part_k, energy_k.at[d - 1], place.along_k(d)) for d in range(1, 2 * nx)]
     wait_all(rows)
     rows = [send(rows_y, rows_k.at[d], place.along_k(d)) for d in range(1, 2 * nx)]
     rows_k[0] = rows_y[...]
+    for b in range(2, samples):
+        sample(b)
     wait_all(energies)
     part_z[...] = total_of(part_k[...], energy_k, 2 * nx - 1)
     energies = [send(part_z, energy_z.at[d - 1], place.along_z(d)) for d in range(1, nz)]
+    for b in range(samples):
+        backward(b, occ_ref, head_w_ref, slope_ref, log_ref, cot_ref, pre_ref)
+    grams(samples, rows_ref, log_ref, rows_t_ref, input_ref, output_ref)
     wait_all(rows)
     spread(place, rows_k, gathered_ref)
     wait_all(energies)
-    total_ref[...] = total_of(part_z[...], energy_z, nz - 1)
-
-
-def gather(nx, ny, nz, rows, energy):
+    total = total_of(part_z[...], energy_z, nz - 1)[0:1]
+    samples_all = samples * 2 * nx * ny * nz
+    mean_energy = total / samples_all
+    weighted_sums(
+        samples,
+        lambda b: (energy_ref[b][0:1] - mean_energy) / samples_all,
+        embedded_ref, pre_ref, rows_t_ref, cot_ref, conv_ref, head_ref,
+    )
+    lay_out(nx, ny, conv_ref, input_ref, head_ref, output_ref, parts_ref)
+
+
+def local_parts(nx, ny, nz, occupations, energy, inverse_tile, embed_weight, conv_weight, head_weight):
     tile = (8, 128)
+    samples = occupations.shape[0]
+    sites = L * L
     copies = 2 * (ny - 1) + 2 * (2 * nx - 1) + nz - 1
+
+    def buffer(*shape, dtype=jnp.float32):
+        return pltpu.VMEM(shape, dtype)
+
     return pl.pallas_call(
-        functools.partial(gather_kernel, nx, ny, nz),
-        name="gather_rows",
+        functools.partial(parts_kernel, nx, ny, nz, samples),
+        name="local_parts",
         out_shape=(
+            jax.ShapeDtypeStruct((2, nx, ny, TILES) + tile, jnp.float32),
             jax.ShapeDtypeStruct((2 * nx, ny) + tile, jnp.float32),
-            jax.ShapeDtypeStruct(tile, jnp.float32),
         ),
-        in_specs=[pl.BlockSpec(memory_space=pltpu.VMEM)] * 2,
+        in_specs=[pl.BlockSpec(memory_space=pltpu.VMEM)] * 7,
         out_specs=[pl.BlockSpec(memory_space=pltpu.VMEM)] * 2,
         scratch_shapes=[
-            pltpu.VMEM((ny,) + tile, jnp.float32),
-            pltpu.VMEM((2 * nx, ny) + tile, jnp.float32),
-            pltpu.VMEM((ny - 1,) + tile, jnp.float32),
-            pltpu.VMEM((2 * nx - 1,) + tile, jnp.float32),
-            pltpu.VMEM((nz - 1,) + tile, jnp.float32),
-            pltpu.VMEM(tile, jnp.float32),
-            pltpu.VMEM(tile, jnp.float32),
+            buffer(ny, *tile),
+            buffer(2 * nx, ny, *tile),
+            buffer(*tile),
+            buffer(ny - 1, *tile),
+            buffer(2 * nx - 1, *tile),
+            buffer(nz - 1, *tile),
+            buffer(*tile),
+            buffer(*tile),
+            buffer(samples, sites, C, dtype=jnp.bfloat16),
+            buffer(samples, sites, C),
+            buffer(samples, NE, C, dtype=jnp.bfloat16),
+            buffer(samples, NE, NE),
+            buffer(samples, NE, NE, dtype=jnp.bfloat16),
+            buffer(samples, sites, C, dtype=jnp.bfloat16),
+            buffer(C, samples * NE, dtype=jnp.bfloat16),
+            buffer(C, C),
+            buffer(NE, NE),
+            buffer(9 * C, C),
+            buffer(C, NE),
             pltpu.SemaphoreType.DMA((copies,)),
             pltpu.SemaphoreType.DMA((copies,)),
         ],
-        compiler_params=pltpu.CompilerParams(collective_id=0, has_side_effects=True),
-    )(rows, energy)
+        compiler_params=pltpu.CompilerParams(
+            collective_id=0, has_side_effects=True, vmem_limit_bytes=48 * 2**20
+        ),
+    )(
+        occupations.reshape(samples, 1, NE),
+        occupations.reshape(samples, NE, 1),
+        energy,
+        inverse_tile,
+        embed_weight,
+        conv_weight,
+        head_weight,
+    )
 
 
 def reduce_kernel(
@@ -154,7 +347,7 @@
     block, block_y, block_k, send_sem, recv_sem,
 ):
     place = Place(nx, ny, nz)
-    place.greet()
+    place.wait_peers(place.signal_peers())
     send = Sender(send_sem, recv_sem)
     order = [*range(1, nx), 0]
     other = 1 - place.c
@@ -237,12 +430,6 @@
     )(parts)
 
 
-def by_place(nx, ny, array, width):
-    rows = array.shape[0] // (2 * nx * ny)
-    split = array.reshape(nx, ny, 2, rows, width // 128, 128)
-    return split.transpose(2, 0, 1, 4, 3, 5).reshape(2, nx, ny, rows * width // 128, 128)
-
-
 def in_order(nx, ny, gathered):
     split = gathered.reshape(nx, 2, ny, gathered.shape[-2], 128)
     return split.transpose(0, 2, 1, 3, 4).reshape(2 * nx * ny, gathered.shape[-2], 128)
@@ -253,82 +440,15 @@
     return jnp.concatenate([rows[..., :half, :], rows[..., half:, :]], axis=-1)
 
 
-def neighbours(lattice):
-    shifted_views = [
-        jnp.roll(lattice, (-shift_x, -shift_y), axis=(1, 2))
-        for shift_x in (-1, 0, 1)
-        for shift_y in (-1, 0, 1)
-    ]
-    return jnp.concatenate(shifted_views, axis=-1)
-
-
-def local_parts(occupations, weights, embed_weight, conv_weight, head_weight):
-    sample_count = occupations.shape[0]
-    site_count = L * L
-    site_ids = jnp.arange(site_count, dtype=jnp.int32)
-    select = (occupations[:, :, None] == site_ids[None, None, :]).astype(jnp.bfloat16)
-    half_count = NE // 2
-    up_fill = jnp.sum(select[:, :half_count].astype(jnp.float32), axis=1)
-    down_fill = jnp.sum(select[:, half_count:].astype(jnp.float32), axis=1)
-    lattice = (
-        jnp.stack([up_fill, down_fill], axis=-1).reshape(sample_count, L, L, 2).astype(jnp.bfloat16)
-    )
-    embed_in = neighbours(lattice).reshape(sample_count * site_count, 18)
-    embedded = jnp.tanh(jnp.dot(embed_in, embed_weight, preferred_element_type=jnp.float32)).astype(
-        jnp.bfloat16
-    )
-    patches = neighbours(embedded.reshape(sample_count, L, L, C)).reshape(
-        sample_count * site_count, 9 * C
-    )
-    conv_pre = jnp.dot(patches, conv_weight, preferred_element_type=jnp.float32)
-    squash = jnp.tanh(conv_pre)
-    hidden = (
-        (embedded.astype(jnp.float32) + squash)
-        .astype(jnp.bfloat16)
-        .reshape(sample_count, site_count, C)
-    )
-    electron_rows = jnp.einsum(
-        "bis,bsc->bic", select, hidden, preferred_element_type=jnp.float32
-    ).astype(jnp.bfloat16)
-    flat_rows = electron_rows.reshape(sample_count * NE, C)
-    logits = jnp.dot(flat_rows, head_weight, preferred_element_type=jnp.float32).reshape(
-        sample_count, NE, NE
-    )
-    orbital_tanh = jnp.tanh(logits)
-    identity = jnp.eye(NE, dtype=jnp.float32)
-    slater_scale = 0.35 / math.sqrt(NE)
-    slater = identity + slater_scale * orbital_tanh
-    inverse_est = 2.0 * identity - slater
-    for sweep in range(NS_STEPS - 1):
-        product = jnp.einsum("bij,bjk->bik", slater, inverse_est, precision=lax.Precision.HIGHEST)
-        inverse_est = jnp.einsum(
-            "bij,bjk->bik", inverse_est, 2.0 * identity - product, precision=lax.Precision.HIGHEST
-        )
-    log_grads = (1.0 - orbital_tanh * orbital_tanh) * jnp.swapaxes(inverse_est, 1, 2)
-    cotangent = (slater_scale * log_grads).astype(jnp.bfloat16)
-    weighted = (weights[:, None, None] * (slater_scale * log_grads)).astype(jnp.bfloat16)
-    head_part = jnp.dot(
-        flat_rows.T, weighted.reshape(sample_count * NE, NE), preferred_element_type=jnp.float32
-    )
-    input_gram = jnp.einsum("nc,nd->cd", flat_rows, flat_rows, preferred_element_type=jnp.float32)
-    flat_grads = log_grads.reshape(sample_count * NE, NE)
-    output_gram = jnp.dot(flat_grads.T, flat_grads, precision=lax.Precision.HIGHEST)
-    row_grads = (
-        jnp.dot(
-            cotangent.reshape(sample_count * NE, NE),
-            head_weight.T,
-            preferred_element_type=jnp.float32,
-        )
-        .astype(jnp.bfloat16)
-        .reshape(sample_count, NE, C)
-    )
-    hidden_grad = jnp.einsum("bis,bic->bsc", select, row_grads, preferred_element_type=jnp.float32)
-    pre_grad = (
-        (weights[:, None, None] * hidden_grad).reshape(sample_count * site_count, C)
-        * (1.0 - squash * squash)
-    ).astype(jnp.bfloat16)
-    conv_part = jnp.dot(patches.T, pre_grad, preferred_element_type=jnp.float32)
-    return conv_part, input_gram, head_part, output_gram
+def rows_of(chunk, aligned, c):
+    main = 8 * aligned
+    edge = jnp.concatenate([chunk[2 * main : 2 * main + 4], chunk[2 * main + 4 : 2 * main + 8]], axis=1)
+    if aligned == 0:
+        return edge
+    inner = jnp.concatenate([chunk[:main], chunk[main : 2 * main]], axis=1)
+    after = jnp.concatenate([inner, edge], axis=0)
+    before = jnp.concatenate([edge, inner], axis=0)
+    return jnp.where(c == 0, after, before)
 
 
 def per_device(
@@ -347,27 +467,16 @@
 ):
     samples_all = occupations.shape[0] * 2 * nx * ny * nz
     inverse_tile = jnp.concatenate([a_inverse[:, :128], a_inverse[:, 128:]], axis=0)
-    energy_tile = jnp.broadcast_to(jnp.sum(local_energy), (8, 128))
-    inverse_tiles, energy_whole = gather(nx, ny, nz, inverse_tile, energy_tile)
-    mean_energy = energy_whole[0, 0] / samples_all
-    weights = (local_energy - mean_energy) / samples_all
-    conv_part, input_gram, head_part, output_gram = local_parts(
-        occupations, weights, embed_weight, conv_weight, head_weight
-    )
-    output_rows = by_place(nx, ny, output_gram, NE)
-    parts = jnp.concatenate(
-        [
-            by_place(nx, ny, conv_part, C),
-            by_place(nx, ny, input_gram, C),
-            by_place(nx, ny, head_part, NE),
-            jnp.pad(output_rows, ((0, 0),) * 3 + ((0, 4 - output_rows.shape[3]), (0, 0))),
-        ],
-        axis=3,
-    ).reshape(2, nx, ny, TILES, 8, 128)
+    energy = jnp.broadcast_to(local_energy[:, None, None], local_energy.shape + (8, 128))
+    embed_padded = jnp.pad(embed_weight, ((0, 128 - embed_weight.shape[0]), (0, 0)))
+    parts, inverse_tiles = local_parts(
+        nx, ny, nz, occupations, energy, inverse_tile, embed_padded, conv_weight, head_weight
+    )
     chunk, gathered = reduce(nx, ny, nz, parts)
     chunk = chunk.reshape(nz * 8, 128)
-    conv_panel = widen(chunk[:72])
-    input_rows = widen(chunk[72:80])
+    core = lax.rem(lax.axis_index("orb"), 2)
+    conv_panel = rows_of(chunk[:72], 4, core)
+    input_rows = rows_of(chunk[72:80], 0, core)
     blocks = in_order(nx, ny, gathered)
     head_grad = blocks[:, 0:4].reshape(C, NE)
     output_sum = blocks[:, 4:6].reshape(NE, NE)

time: 156 us -> 117 us (0.75)
  local copies, waits for them, and re-layouts: 30.1 us -> 10.8 us
  matrix products: 13.8 us -> 1.24 us
  other arithmetic: 9.52 us -> 3.24 us
    dot_general x5 -> x0, local copies, waits for them, and re-layouts: 16.1 us -> none  [the longest x3 14.2 us: local_parts(): conv_part = jnp.dot(patches.T, pre_grad, preferred_element_type=jnp.float32)]
    dot_general x14 -> x0, matrix products: 12.6 us -> none  [the longest x1 3.76 us: local_parts(): conv_part = jnp.dot(patches.T, pre_grad, preferred_element_type=jnp.float32)]
    concatenate x21 -> x0, other arithmetic: 3.75 us -> none  [the longest x20 2.54 us: neighbours(): jnp.roll(lattice, (-shift_x, -shift_y), axis=(1, 2))]
    unnamed x37 -> x14, local copies, waits for them, and re-layouts: 1.05 us -> 4.39 us
    concatenate x11 -> x0, local copies, waits for them, and re-layouts: 3.02 us -> none  [the longest x1 2.07 us: per_device(): jnp.concatenate([by_place(nx, ny, conv_part, C), by_place(nx, ny, input_g...]
    transpose x2 -> x0, local copies, waits for them, and re-layouts: 2.11 us -> none  [by_place(): split.transpose(2, 0, 1, 4, 3, 5)]
where the time goes in v2:
time: 117 us; the launch traced here: 116 us
  Pallas kernels  98.9 us (85%)
  local copies, waits for them, and re-layouts  10.8 us (9%)
  other arithmetic  3.24 us (3%)
  between operations  2.24 us (2%)
  matrix products  1.24 us (1%)
    pallas_call x1, Pallas kernels, reduce(): pl.pallas_call(functools.partial(reduce_kernel, nx, ny, nz), name='reduce...  62 us
    pallas_call x1, Pallas kernels, local_parts(): pl.pallas_call(functools.partial(parts_kernel, nx, ny, nz, samples), name...  36.9 us
    unnamed x14, local copies, waits for them, and re-layouts  4.39 us

profile of v2, /device:TPU:1, one launch (start us, length us, event | category | flops | bytes accessed | tf_op | source)
XLA Modules:
  0.0 116.4 jit_solution(9658679395149541493)
XLA Ops:
  0.6 0.0 copy-start
  0.6 0.7 fusion.4
  1.4 0.8 copy.13.occ_t_ref
  2.2 0.7 pad.4.embed_ref
  2.9 0.7 broadcast_in_dim.2.energy_ref
  3.7 0.0 copy-start.2
  3.7 1.3 %copy-done.2 = bf16[2304,256]{1,0:T(8,128)(2,1)S(1)} copy-done((bf16[2304,256]{1,0:T(8,128)(2,1)S(1)}, bf16[2304,256]{1,0:T(8,128)(2,1)}, u32[]{:S(2)}) %copy-start.2) | copy-done | bytes 1179672
  4.9 0.0 copy-start.3
  4.9 0.8 copy-done.3
  5.8 0.7 copy-done.4
  6.5 36.9 %local_parts.1 = (f32[2,4,8,11,8,128]{5,4,3,2,1,0:T(8,128)S(1)}, f32[8,8,8,128]{3,2,1,0:T(8,128)S(1)}) custom-call(s32[4,1,128]{2,1,0:T(1,128)S(1)} %bitcast.28, s32[4,128,1]{2,1,0:T(8,128)S(1)} %copy.13.occ_t_ref, f32[4,8,128]{2,1,0:T(8,128)S(1)} %broadcast_in_dim.2.energy_ref, f32[8,128]{1,0:T(8,128)S(1)} %pad_maximum_fusion.1.inverse_ref, ...), custom_call_target="tpu_custom_call" | custom-call | tf_op jit(solution)/shard_map/local_parts/pallas_call | solution.py:298
  43.4 0.0 copy-start.1
  43.4 1.6 %copy-done.1 = f32[2,4,8,11,8,128]{5,4,3,2,1,0:T(8,128)} copy-done((f32[2,4,8,11,8,128]{5,4,3,2,1,0:T(8,128)}, f32[2,4,8,11,8,128]{5,4,3,2,1,0:T(8,128)S(1)}, u32[]{:S(2)}) %copy-start.1) | copy-done | bytes 2883608
  45.0 0.1 pad_maximum_fusion
  45.1 0.0 copy-start.6
  45.1 0.0 copy-start.5
  45.1 0.1 reshape.47
  45.2 62.0 %reduce_parts.1 = (f32[12,8,128]{2,1,0:T(8,128)}, f32[8,8,8,128]{3,2,1,0:T(8,128)}) custom-call(f32[2,4,8,11,8,128]{5,4,3,2,1,0:T(8,128)} %copy-done.1), custom_call_target="tpu_custom_call" | custom-call | tf_op jit(solution)/shard_map/reduce_parts/pallas_call | solution.py:404
  107.2 1.0 copy.15
  108.2 0.4 fusion.5
  108.6 0.0 copy-done
  108.6 0.9 multiply_reduce_fusion
  110.2 0.6 dynamic-slice_multiply_fusion
  110.8 0.8 slice_bitcast_fusion
  111.6 0.7 slice_bitcast_fusion.2
  112.3 0.7 slice_reduce_fusion
  113.7 0.6 fusion
  114.4 0.8 slice_bitcast_fusion.4
  115.1 0.0 copy-done.6
  115.1 0.6 fusion.1
  115.8 0.0 copy-done.5
  115.8 0.6 multiply_add_fusion
  (7 shorter events, 0.1 us)
Async XLA Ops:
  0.6 108.0 %copy-start = (f32[128,128]{1,0:T(8,128)S(1)}, f32[128,128]{1,0:T(8,128)}, u32[]{:S(2)}) copy-start(f32[128,128]{1,0:T(8,128)} %param.17) | copy-start | bytes 196612
  3.7 1.3 %copy-start.2 = (bf16[2304,256]{1,0:T(8,128)(2,1)S(1)}, bf16[2304,256]{1,0:T(8,128)(2,1)}, u32[]{:S(2)}) copy-start(bf16[2304,256]{1,0:T(8,128)(2,1)} %conv_w_ref.1) | copy-start | bytes 3538948
  4.9 0.8 copy-start.3
  5.8 0.7 copy-start.4
  43.4 1.6 %copy-start.1 = (f32[2,4,8,11,8,128]{5,4,3,2,1,0:T(8,128)}, f32[2,4,8,11,8,128]{5,4,3,2,1,0:T(8,128)S(1)}, u32[]{:S(2)}) copy-start(f32[2,4,8,11,8,128]{5,4,3,2,1,0:T(8,128)S(1)} %get-tuple-element.9.parts_ref) | copy-start | bytes 8650756
  45.1 70.0 %copy-start.6 = (f32[4,256]{1,0:T(4,128)S(1)}, f32[4,256]{1,0:T(4,128)}, u32[]{:S(2)}) copy-start(f32[4,256]{1,0:T(4,128)} %param.14) | copy-start | bytes 12292
  45.1 70.6 %copy-start.5 = (f32[128,128]{1,0:T(8,128)S(1)}, f32[128,128]{1,0:T(8,128)}, u32[]{:S(2)}) copy-start(f32[128,128]{1,0:T(8,128)} %param.15) | copy-start | bytes 196612

commit v3 on v2

v3 whole, which is shorter than its diff:
```python
import functools
import math

import jax
import jax.numpy as jnp
from jax import lax
from jax.experimental import pallas as pl
from jax.experimental.pallas import tpu as pltpu
from jax.sharding import PartitionSpec as P

L = 16
C = 256
NS_STEPS = 3
NE = 128
X_CHIPS = 4
TILES = 11
HALF = 6

decay_rate = 0.8
MESH = pl.DeviceIdType.MESH


class Place:
    def __init__(self, nx, ny, nz):
        self.nx, self.ny, self.nz = nx, ny, nz
        self.z = lax.axis_index("walker")
        self.orb = lax.axis_index("orb")
        self.c = lax.rem(self.orb, 2)
        self.y = lax.rem(lax.div(self.orb, 2), ny)
        self.x = lax.div(self.orb, 2 * ny)
        self.k = self.x * 2 + self.c

    def at(self, x, y, c):
        return (self.z, (x * self.ny + y) * 2 + c)

    def core(self):
        return self.at(self.x, self.y, 1 - self.c)

    def along_x(self, d):
        return self.at(lax.rem(self.x + d, self.nx), self.y, self.c)

    def along_y(self, d):
        return self.at(self.x, lax.rem(self.y + d, self.ny), self.c)

    def along_k(self, d):
        k = lax.rem(self.k + d, 2 * self.nx)
        return self.at(lax.div(k, 2), self.y, lax.rem(k, 2))

    def along_z(self, d):
        return (lax.rem(self.z + d, self.nz), self.orb)

    def signal_peers(self):
        barrier = pltpu.get_barrier_semaphore()
        peers = [self.along_y(d) for d in range(1, self.ny)]
        peers += [self.along_k(d) for d in range(1, 2 * self.nx)]
        peers += [self.along_z(d) for d in range(1, self.nz)]
        for peer in peers:
            pl.semaphore_signal(barrier, inc=1, device_id=peer, device_id_type=MESH)
        return len(peers)

    def wait_peers(self, count):
        pl.semaphore_wait(pltpu.get_barrier_semaphore(), count)


class Sender:
    def __init__(self, send_sem, recv_sem):
        self.send_sem, self.recv_sem, self.used = send_sem, recv_sem, 0

    def __call__(self, source, target, device):
        copy = pltpu.make_async_remote_copy(
            src_ref=source,
            dst_ref=target,
            send_sem=self.send_sem.at[self.used],
            recv_sem=self.recv_sem.at[self.used],
            device_id=device,
            device_id_type=MESH,
        )
        copy.start()
        self.used += 1
        return copy


def wait_all(copies):
    for copy in copies:
        copy.wait()


def total_of(first, ref, count):
    total = first
    for i in range(count):
        total = total + ref[i]
    return total


def spread(place, slots_ref, out_ref):
    for i in range(2 * place.nx):
        k = lax.rem(place.k - i + 2 * place.nx, 2 * place.nx)
        for j in range(place.ny):
            y = lax.rem(place.y - j + place.ny, place.ny)
            out_ref[k, y] = slots_ref[i, j]


def site_shift_y(field, b):
    if b == 0:
        return field
    y = lax.broadcasted_iota(jnp.int32, field.shape, 0) & (L - 1)
    sites = field.shape[0]
    if b == 1:
        edge, inside = pltpu.roll(field, L - 1, 0), pltpu.roll(field, sites - 1, 0)
        return jnp.where(y == L - 1, edge, inside)
    edge, inside = pltpu.roll(field, sites - L + 1, 0), pltpu.roll(field, 1, 0)
    return jnp.where(y == 0, edge, inside)


def site_shift_x(field, a):
    if a == 0:
        return field
    cut = L if a == 1 else field.shape[0] - L
    return jnp.concatenate([field[cut:], field[:cut]], axis=0)


def site_patches(field, sign):
    by_y = {b: site_shift_y(field, sign * b).astype(jnp.bfloat16) for b in (-1, 0, 1)}
    return jnp.concatenate(
        [site_shift_x(by_y[b], sign * a) for a in (-1, 0, 1) for b in (-1, 0, 1)], axis=1
    )


def multiply(left, right):
    return jnp.dot(
        left.astype(jnp.bfloat16), right.astype(jnp.bfloat16), preferred_element_type=jnp.float32
    )


def electrons_by_site(occ_ref, b):
    sites = lax.broadcasted_iota(jnp.int32, (L * L, NE), 0)
    return (sites == occ_ref[b : b + 1, :]).astype(jnp.float32)


def forward(b, occ_ref, embed_ref, conv_w_ref, head_w_ref,
            embedded_ref, slope_ref, rows_ref, log_ref):
    by_site = electrons_by_site(occ_ref, b)
    electron = lax.broadcasted_iota(jnp.int32, (NE, 128), 0)
    lane = lax.broadcasted_iota(jnp.int32, (NE, 128), 1)
    down = (electron >= NE // 2).astype(jnp.int32)
    spin = ((lane & 1) == down).astype(jnp.float32)
    counts = multiply(by_site, spin)
    tap_of_lane = lax.broadcasted_iota(jnp.int32, counts.shape, 1) >> 1
    near = jnp.zeros_like(counts)
    for j in (-1, 0, 1):
        at_y = site_shift_y(counts, j)
        for i in (-1, 0, 1):
            tap = (i + 1) * 3 + j + 1
            near = jnp.where(tap_of_lane == tap, site_shift_x(at_y, i), near)
    embedded = jnp.tanh(multiply(near[:, : embed_ref.shape[0]], embed_ref[...])).astype(jnp.bfloat16)
    embedded_ref[b] = embedded
    wide = embedded.astype(jnp.float32)
    squash = jnp.tanh(multiply(site_patches(wide, 1), conv_w_ref[...]))
    slope_ref[b] = 1.0 - squash * squash
    hidden = (wide + squash).astype(jnp.bfloat16)
    rows = multiply(by_site.T, hidden).astype(jnp.bfloat16)
    rows_ref[b] = rows
    orbital_tanh = jnp.tanh(multiply(rows, head_w_ref[...]))
    shift = (0.35 / math.sqrt(NE)) * orbital_tanh
    row = lax.broadcasted_iota(jnp.int32, (NE, NE), 0)
    column = lax.broadcasted_iota(jnp.int32, (NE, NE), 1)
    identity = (row == column).astype(jnp.float32)
    second = multiply(shift, shift)
    inverse_est = identity - shift + second - multiply(shift, second)
    inverse_est = inverse_est + multiply(inverse_est, multiply(second, second))
    log_ref[b] = (1.0 - orbital_tanh * orbital_tanh) * inverse_est.T


def backward(b, occ_ref, head_w_ref, slope_ref, log_ref, cot_ref, pre_ref):
    cotangent = ((0.35 / math.sqrt(NE)) * log_ref[b]).astype(jnp.bfloat16)
    cot_ref[b] = cotangent
    row_grads = lax.dot_general(
        cotangent, head_w_ref[...], (((1,), (1,)), ((), ())), preferred_element_type=jnp.float32
    ).astype(jnp.bfloat16)
    hidden_grad = multiply(electrons_by_site(occ_ref, b), row_grads)
    pre_ref[b] = (hidden_grad * slope_ref[b]).astype(jnp.bfloat16)


def grams(samples, rows_ref, log_ref, rows_t_ref, input_ref, output_ref):
    rows = rows_ref[...].reshape(samples * NE, C)
    rows_t = rows.astype(jnp.float32).T.astype(jnp.bfloat16)
    rows_t_ref[...] = rows_t
    input_ref[...] = multiply(rows_t, rows)
    logs = log_ref[...].reshape(samples * NE, NE)
    output_ref[...] = jnp.dot(
        logs.T, logs, precision=lax.Precision.HIGHEST, preferred_element_type=jnp.float32
    )


def weighted_sums(samples, weight_of, embedded_ref, pre_ref, rows_t_ref, cot_ref, conv_ref, head_ref):
    for b in range(samples):
        weight = weight_of(b)
        wide = jnp.concatenate([weight, weight], axis=1)
        embedded_t = embedded_ref[b].astype(jnp.float32).T
        terms = multiply(embedded_t, site_patches(pre_ref[b].astype(jnp.float32), -1))
        head = weight * multiply(rows_t_ref[:, b * NE : (b + 1) * NE], cot_ref[b])
        head_ref[...] = head if b == 0 else head_ref[...] + head
        for tap in range(9):
            rows = slice(tap * C, (tap + 1) * C)
            term = wide * terms[:, rows]
            conv_ref[rows, :] = term if b == 0 else conv_ref[rows, :] + term


def lay_out(nx, ny, conv_ref, input_ref, head_ref, output_ref, parts_ref):
    row = lax.broadcasted_iota(jnp.int32, (8, 128), 0)

    def halves(first, second, c):
        if c == 0:
            return jnp.where(row < 4, first, pltpu.roll(second, 4, 0))
        return jnp.where(row < 4, pltpu.roll(first, 4, 0), second)

    for pair in range(nx * ny):
        x, y = pair // ny, pair % ny
        for c in range(2):
            top = 72 * pair + 40 * c
            for half in range(2):
                lanes = slice(128 * half, 128 * half + 128)
                for i in range(4):
                    tile = conv_ref[top + 8 * i : top + 8 * i + 8, lanes]
                    parts_ref[c, x, y, 4 * half + i] = tile
            middle = slice(72 * pair + 32, 72 * pair + 40)
            parts_ref[c, x, y, 8] = halves(conv_ref[middle, :128], conv_ref[middle, 128:], c)
            eight = slice(8 * pair, 8 * pair + 8)
            parts_ref[c, x, y, 9] = halves(input_ref[eight, :128], input_ref[eight, 128:], c)
            place = 4 * (pair % 2) + 2 * c
            output = output_ref[8 * (pair // 2) : 8 * (pair // 2) + 8, :]
            output = pltpu.roll(output, (4 - place) % 8, 0) if place != 4 else output
            head = head_ref[eight, :] if c == 0 else pltpu.roll(head_ref[eight, :], 4, 0)
            parts_ref[c, x, y, 10] = jnp.where(row < 4, head, output)


def row_index():
    return lax.broadcasted_iota(jnp.int32, (8, 128), 0)


def inverse_from(nx, ny, gathered_ref, inverse_ref):
    row = row_index()
    for pair in range(nx * ny):
        x, y = pair // ny, pair % ny
        first, second = gathered_ref[2 * x, y], gathered_ref[2 * x + 1, y]
        eight = slice(8 * pair, 8 * pair + 8)
        inverse_ref[eight, :128] = jnp.where(row < 4, first, pltpu.roll(second, 4, 0))
        inverse_ref[eight, 128:] = jnp.where(row < 4, pltpu.roll(first, 4, 0), second)


def head_from(nx, ny, gathered_ref, head_ref, output_ref):
    row = row_index()
    squares = jnp.zeros((8, 128), jnp.float32)
    for pair in range(0, nx * ny, 2):
        tiles = []
        for p in (pair, pair + 1):
            x, y = p // ny, p % ny
            first, second = gathered_ref[2 * x, y], gathered_ref[2 * x + 1, y]
            head_ref[8 * p : 8 * p + 8, :] = jnp.where(row < 4, first, pltpu.roll(second, 4, 0))
            squares = squares + (first + second)
            tiles += [first, second]
        upper = jnp.where(row < 2, pltpu.roll(tiles[0], 4, 0), pltpu.roll(tiles[1], 6, 0))
        lower = jnp.where(row < 6, tiles[2], pltpu.roll(tiles[3], 2, 0))
        output_ref[4 * pair : 4 * pair + 8, :] = jnp.where(row < 4, upper, lower)
    return jnp.sum(squares[6:7], axis=1, keepdims=True)


def exchange(
    place, send, parts_ref, chunk_ref, gathered_ref,
    from_core, sum_core, relay_up, relay_down, from_x, sum_x, from_y, sum_y, from_z, sum_z, got_z,
    block, block_y, block_k,
):
    nx, ny, nz = place.nx, place.ny, place.nz
    order = sorted(range(1, ny), key=lambda d: -min(d, ny - d)) + [0]
    at_x = [lax.rem(place.x + d, nx) for d in range(nx)]
    at_y = [lax.rem(place.y + d, ny) for d in range(ny)]
    low, high = pl.ds(0, HALF), pl.ds(HALF, TILES - HALF)
    core, relays, across, along = {}, {}, {}, []
    for d in order:
        source = parts_ref.at[1 - place.c, :, at_y[d]]
        core[d] = send(source, from_core.at[:, at_y[d]], place.core())
    for d in order:
        core[d].wait()
        sum_core[:, at_y[d]] = parts_ref[place.c, :, at_y[d]] + from_core[:, at_y[d]]
        relays[d] = [
            send(sum_core.at[at_x[2], at_y[d], low], relay_up.at[d], place.along_x(1)),
            send(sum_core.at[at_x[2], at_y[d], high], relay_down.at[d], place.along_x(nx - 1)),
        ]
    for d in order:
        wait_all(relays[d])
        sum_core[at_x[1], at_y[d], low] = sum_core[at_x[1], at_y[d], low] + relay_up[d]
        sum_core[at_x[3], at_y[d], high] = sum_core[at_x[3], at_y[d], high] + relay_down[d]
        across[d] = [
            send(sum_core.at[at_x[1], at_y[d]], from_x.at[0, d], place.along_x(1)),
            send(sum_core.at[at_x[3], at_y[d]], from_x.at[1, d], place.along_x(nx - 1)),
        ]
    for d in order:
        wait_all(across[d])
        sum_x[d] = sum_core[place.x, at_y[d]] + (from_x[0, d] + from_x[1, d])
        if d:
            along.append(send(sum_x.at[d], from_y.at[d - 1], place.along_y(d)))
    wait_all(along)
    sum_y[TILES:nz] = jnp.zeros((nz - TILES, 8, 128), jnp.float32)
    sum_y[0:TILES] = total_of(sum_x[0], from_y, ny - 1)
    wait_all(
        [
            send(sum_y.at[lax.rem(place.z + d, nz)], from_z.at[d - 1], place.along_z(d))
            for d in range(1, nz)
        ]
    )
    sum_z[...] = total_of(sum_y[place.z], from_z, nz - 1)
    copies = [send(sum_z, got_z.at[d], place.along_z(d)) for d in range(1, nz)]
    chunk_ref[place.z] = sum_z[...]
    wait_all(copies)
    for d in range(1, nz):
        chunk_ref[lax.rem(place.z - d + nz, nz)] = got_z[d]
    conv = chunk_ref[0:9]
    squares = jnp.sum(jnp.sum(conv * conv, axis=0), axis=0, keepdims=True)
    block[...] = jnp.where(
        row_index() == 6, jnp.broadcast_to(squares, (8, 128)), chunk_ref[TILES - 1]
    )
    copies = [send(block, block_y.at[d], place.along_y(d)) for d in range(1, ny)]
    block_y[0] = block[...]
    wait_all(copies)
    copies = [send(block_y, block_k.at[d], place.along_k(d)) for d in range(1, 2 * nx)]
    block_k[0] = block_y[...]
    wait_all(copies)
    spread(place, block_k, gathered_ref)


def dot_highest(left, right):
    return jnp.dot(
        left, right, precision=lax.Precision.HIGHEST, preferred_element_type=jnp.float32
    )


def updates(
    place, samples_all, chunk_ref, gathered_ref, a_factor_ref, g_factor_ref, g_inverse_ref,
    inverse_ref, head_ref, output_ref, precond_ref,
    head_update_ref, conv_update_ref, new_a_ref, new_g_ref,
):
    conv_norm = head_from(place.nx, place.ny, gathered_ref, head_ref, output_ref)
    head_grad = head_ref[...]
    precond = dot_highest(dot_highest(inverse_ref[...], head_grad), g_inverse_ref[...])
    precond_ref[...] = precond
    head_norm = jnp.sum(
        jnp.sum(precond * head_grad, axis=0, keepdims=True), axis=1, keepdims=True
    )
    head_scale = -jnp.sqrt(C * NE / 4.0 / head_norm)
    conv_scale = -jnp.sqrt(9 * C * C / 4.0 / conv_norm)
    pair = pl.multiple_of(lax.div(place.orb, 2) * 8, 8)
    eight = head_scale * precond_ref[pl.ds(pair, 8), :]
    head_update_ref[...] = jnp.where(place.c == 0, eight, pltpu.roll(eight, 4, 0))[0:4]
    keep = 1.0 - decay_rate
    for half in range(2):
        lanes = slice(128 * half, 128 * half + 128)
        rows = slice(4 * half, 4 * half + 4)
        input_rows = chunk_ref[9][rows]
        new_a_ref[:, lanes] = (
            decay_rate * a_factor_ref[:, lanes] + keep * input_rows / (samples_all * NE)
        )
        inner = conv_scale * chunk_ref[4 * half : 4 * half + 4].reshape(32, 128)
        edge = conv_scale * chunk_ref[8][rows]

        @pl.when(place.c == 0)
        def _(lanes=lanes, inner=inner, edge=edge):
            conv_update_ref[0:32, lanes] = inner
            conv_update_ref[32:36, lanes] = edge

        @pl.when(place.c == 1)
        def _(lanes=lanes, inner=inner, edge=edge):
            conv_update_ref[0:4, lanes] = edge
            conv_update_ref[4:36, lanes] = inner

    new_g_ref[...] = decay_rate * g_factor_ref[...] + keep * output_ref[...] / samples_all


def step_kernel(
    nx, ny, nz, samples,
    occ_in, energy_in, a_inverse_in, embed_in, conv_w_in, head_w_in,
    a_factor_in, g_factor_in, g_inverse_in,
    head_update_ref, conv_update_ref, new_a_ref, new_g_ref,
    occ_ref, energy_ref, a_inverse_ref, embed_ref, conv_w_ref, head_w_ref,
    a_factor_ref, g_factor_ref, g_inverse_ref,
    rows_own, rows_y, rows_k, energy_own, energy_y, energy_k, energy_z, part_k, part_z,
    embedded_ref, slope_ref, rows_ref, log_ref, cot_ref, pre_ref, rows_t_ref,
    input_ref, output_ref, conv_ref, head_ref, parts_ref, gathered_ref, inverse_ref, precond_ref,
    chunk_ref, *rest,
):
    *buffers, load_sem, send_sem, recv_sem = rest
    place = Place(nx, ny, nz)
    peers = place.signal_peers()
    loads = [
        pltpu.make_async_copy(source, target, load_sem.at[i])
        for i, (source, target) in enumerate(
            [
                (occ_in, occ_ref),
                (energy_in, energy_ref),
                (a_inverse_in, a_inverse_ref),
                (embed_in, embed_ref),
                (conv_w_in, conv_w_ref),
                (head_w_in, head_w_ref),
                (a_factor_in, a_factor_ref),
                (g_factor_in, g_factor_ref),
                (g_inverse_in, g_inverse_ref),
            ]
        )
    ]
    for load in loads:
        load.start()
    send = Sender(send_sem, recv_sem)

    def energy_of(b):
        return jnp.broadcast_to(energy_ref[0:1, b : b + 1], (8, 128))

    def sample(b):
        forward(b, occ_ref, embed_ref, conv_w_ref, head_w_ref,
                embedded_ref, slope_ref, rows_ref, log_ref)

    wait_all(loads[:6])
    energy_own[...] = sum((energy_of(b) for b in range(1, samples)), energy_of(0))
    rows_own[0:4, :] = a_inverse_ref[:, :128]
    rows_own[4:8, :] = a_inverse_ref[:, 128:]
    sample(0)
    place.wait_peers(peers)
    energies = [send(energy_own, energy_y.at[d - 1], place.along_y(d)) for d in range(1, ny)]
    rows = [send(rows_own, rows_y.at[d], place.along_y(d)) for d in range(1, ny)]
    rows_y[0] = rows_own[...]
    sample(1)
    wait_all(energies)
    part_k[...] = total_of(energy_own[...], energy_y, ny - 1)
    energies = [send(part_k, energy_k.at[d - 1], place.along_k(d)) for d in range(1, 2 * nx)]
    wait_all(rows)
    rows = [send(rows_y, rows_k.at[d], place.along_k(d)) for d in range(1, 2 * nx)]
    rows_k[0] = rows_y[...]
    for b in range(2, samples):
        sample(b)
    wait_all(energies)
    part_z[...] = total_of(part_k[...], energy_k, 2 * nx - 1)
    energies = [send(part_z, energy_z.at[d - 1], place.along_z(d)) for d in range(1, nz)]
    for b in range(samples):
        backward(b, occ_ref, head_w_ref, slope_ref, log_ref, cot_ref, pre_ref)
    grams(samples, rows_ref, log_ref, rows_t_ref, input_ref, output_ref)
    wait_all(rows)
    spread(place, rows_k, gathered_ref)
    inverse_from(nx, ny, gathered_ref, inverse_ref)
    wait_all(energies)
    total = total_of(part_z[...], energy_z, nz - 1)[0:1]
    samples_all = samples * 2 * nx * ny * nz
    mean_energy = total / samples_all
    weighted_sums(
        samples,
        lambda b: (energy_of(b)[0:1] - mean_energy) / samples_all,
        embedded_ref, pre_ref, rows_t_ref, cot_ref, conv_ref, head_ref,
    )
    lay_out(nx, ny, conv_ref, input_ref, head_ref, output_ref, parts_ref)
    wait_all(loads[6:])
    exchange(place, send, parts_ref, chunk_ref, gathered_ref, *buffers)
    updates(
        place, samples_all, chunk_ref, gathered_ref, a_factor_ref, g_factor_ref, g_inverse_ref,
        inverse_ref, head_ref, output_ref, precond_ref,
        head_update_ref, conv_update_ref, new_a_ref, new_g_ref,
    )


def per_device(
    nx,
    ny,
    nz,
    occupations,
    local_energy,
    embed_weight,
    conv_weight,
    head_weight,
    a_factor,
    g_factor,
    a_inverse,
    g_inverse,
):
    samples = occupations.shape[0]
    sites = L * L
    orb = 2 * nx * ny
    copies = 2 * (ny - 1) + 2 * (2 * nx - 1) + nz - 1
    copies += 5 * ny + 2 * (ny - 1) + 2 * (nz - 1) + 2 * nx - 1

    inputs = (
        occupations,
        local_energy.reshape(1, samples),
        a_inverse,
        embed_weight,
        conv_weight,
        head_weight,
        a_factor,
        g_factor,
        g_inverse,
    )

    def buffer(*shape, dtype=jnp.float32):
        return pltpu.VMEM(shape, dtype)

    def tiles(*lead):
        return pltpu.VMEM(lead + (8, 128), jnp.float32)

    return pl.pallas_call(
        functools.partial(step_kernel, nx, ny, nz, samples),
        name="natural_step",
        out_shape=(
            jax.ShapeDtypeStruct((C // orb, NE), jnp.float32),
            jax.ShapeDtypeStruct((9 * C // orb, C), jnp.float32),
            jax.ShapeDtypeStruct((C // orb, C), jnp.float32),
            jax.ShapeDtypeStruct((NE, NE), jnp.float32),
        ),
        in_specs=[pl.BlockSpec(memory_space=pl.ANY)] * 9,
        out_specs=[pl.BlockSpec(memory_space=pltpu.VMEM)] * 4,
        scratch_shapes=[pltpu.VMEM(a.shape, a.dtype) for a in inputs]
        + [
            tiles(),
            tiles(ny),
            tiles(2 * nx, ny),
            tiles(),
            tiles(ny - 1),
            tiles(2 * nx - 1),
            tiles(nz - 1),
            tiles(),
            tiles(),
            buffer(samples, sites, C, dtype=jnp.bfloat16),
            buffer(samples, sites, C),
            buffer(samples, NE, C, dtype=jnp.bfloat16),
            buffer(samples, NE, NE),
            buffer(samples, NE, NE, dtype=jnp.bfloat16),
            buffer(samples, sites, C, dtype=jnp.bfloat16),
            buffer(C, samples * NE, dtype=jnp.bfloat16),
            buffer(C, C),
            buffer(NE, NE),
            buffer(9 * C, C),
            buffer(C, NE),
            tiles(2, nx, ny, TILES),
            tiles(2 * nx, ny),
            buffer(C, C),
            buffer(C, NE),
            tiles(nz),
            tiles(nx, ny, TILES),
            tiles(nx, ny, TILES),
            tiles(ny, HALF),
            tiles(ny, TILES - HALF),
            tiles(2, ny, TILES),
            tiles(ny, TILES),
            tiles(ny - 1, TILES),
            tiles(nz),
            tiles(nz - 1),
            tiles(),
            tiles(nz),
            tiles(),
            tiles(ny),
            tiles(2 * nx, ny),
            pltpu.SemaphoreType.DMA((len(inputs),)),
            pltpu.SemaphoreType.DMA((copies,)),
            pltpu.SemaphoreType.DMA((copies,)),
        ],
        compiler_params=pltpu.CompilerParams(collective_id=0, has_side_effects=True),
    )(*inputs)


def solution(mesh):
    nz, orb = mesh.shape["walker"], mesh.shape["orb"]
    in_specs = (
        P(("walker", "orb"), None),
        P(("walker", "orb")),
        P(),
        P(),
        P(),
        P("orb", None),
        P(),
        P("orb", None),
        P(),
    )
    out_specs = (P("orb", None), P("orb", None), P("orb", None), P())
    return jax.shard_map(
        functools.partial(per_device, X_CHIPS, orb // (2 * X_CHIPS), nz),
        mesh=mesh,
        in_specs=in_specs,
        out_specs=out_specs,
        check_vma=False,
    )
```

time: 117 us -> 87.2 us (0.75)
  Pallas kernels: 98.9 us -> 80.9 us
  local copies, waits for them, and re-layouts: 10.8 us -> 5.4 us
  other arithmetic: 3.24 us -> 0 us
  between operations: 2.24 us -> 0.64 us
  matrix products: 1.24 us -> 0 us
    pallas_call x2 -> x1, Pallas kernels: 98.9 us -> 80.9 us  [per_device(): pl.pallas_call(functools.partial(step_kernel, nx, ny, nz, samples), name=...]
    slice x7 -> x0, local copies, waits for them, and re-layouts: 3.07 us -> none  [the longest x1 0.77 us: per_device(): conv_panel = rows_of(chunk[:72], 4, core)]
    reshape x4 -> x0, local copies, waits for them, and re-layouts: 1.9 us -> none  [the longest x2 0.99 us: in_order(): split = gathered.reshape(nx, 2, ny, gathered.shape[-2], 128)]
    add x2 -> x0, other arithmetic: 1.24 us -> none  [the longest x1 0.64 us: per_device(): decay_rate * g_factor + (1.0 - decay_rate) * output_sum / samples_all]
    dot_general x2 -> x0, matrix products: 1.24 us -> none  [the longest x1 0.86 us: per_device(): precond = jnp.dot(left_applied, g_inverse, precision=lax.Precision.HIGHEST)]
    mul x2 -> x0, other arithmetic: 1.22 us -> none  [the longest x1 0.63 us: per_device(): conv_update = -jnp.sqrt(9 * C * C / 4.0 / conv_norm) * conv_panel]
    unnamed x14 -> x4, local copies, waits for them, and re-layouts: 4.39 us -> 5.4 us
where the time goes in v3:
time: 87.2 us; the launch traced here: 86.9 us
  Pallas kernels  80.9 us (93%)
  local copies, waits for them, and re-layouts  5.4 us (6%)
    pallas_call x1, Pallas kernels, per_device(): pl.pallas_call(functools.partial(step_kernel, nx, ny, nz, samples), name=...  80.9 us
    unnamed x4, local copies, waits for them, and re-layouts  5.4 us

profile of v3, /device:TPU:1, one launch (start us, length us, event | category | flops | bytes accessed | tf_op | source)
XLA Modules:
  0.0 86.9 jit_solution(13245325086297109677)
XLA Ops:
  0.6 80.9 %natural_step.1 = (f32[4,128]{1,0:T(4,128)}, f32[36,256]{1,0:T(8,128)}, f32[4,256]{1,0:T(4,128)}, f32[128,128]{1,0:T(8,128)}) custom-call(s32[4,128]{1,0:T(4,128)} %occ_in.1, f32[1,4]{1,0:T(1,128)} %bitcast.1, f32[4,256]{1,0:T(4,128)} %a_inverse_in.1, bf16[18,256]{1,0:T(8,128)(2,1)} %embed_in.1, bf16[2304,256]{1,0:T(8,128)(2,1)} %conv_w_in.1, ...), custom_call_target="tpu_custom_call" | custom-call | tf_op jit(solution)/shard_map/natural_step/pallas_call | solution.py:504
  81.5 1.3 %copy.17 = f32[4,128]{1,0:T(4,128)} copy(f32[4,128]{1,0:T(4,128)} %get-tuple-element.8) | data formatting | bytes 4096
  82.8 1.4 %copy.18 = f32[36,256]{1,0:T(8,128)} copy(f32[36,256]{1,0:T(8,128)} %get-tuple-element.9) | data formatting | bytes 73728
  84.2 1.3 %copy.19 = f32[4,256]{1,0:T(4,128)} copy(f32[4,256]{1,0:T(4,128)} %get-tuple-element.10) | data formatting | bytes 8192
  85.5 1.5 %copy.20 = f32[128,128]{1,0:T(8,128)} copy(f32[128,128]{1,0:T(8,128)} %get-tuple-element.11) | data formatting | bytes 131072

commit v4 on v3

--- a/solution.py
+++ b/solution.py
@@ -250,25 +250,22 @@
 
 def head_from(nx, ny, gathered_ref, head_ref, output_ref):
     row = row_index()
-    squares = jnp.zeros((8, 128), jnp.float32)
     for pair in range(0, nx * ny, 2):
         tiles = []
         for p in (pair, pair + 1):
             x, y = p // ny, p % ny
             first, second = gathered_ref[2 * x, y], gathered_ref[2 * x + 1, y]
             head_ref[8 * p : 8 * p + 8, :] = jnp.where(row < 4, first, pltpu.roll(second, 4, 0))
-            squares = squares + (first + second)
             tiles += [first, second]
         upper = jnp.where(row < 2, pltpu.roll(tiles[0], 4, 0), pltpu.roll(tiles[1], 6, 0))
         lower = jnp.where(row < 6, tiles[2], pltpu.roll(tiles[3], 2, 0))
         output_ref[4 * pair : 4 * pair + 8, :] = jnp.where(row < 4, upper, lower)
-    return jnp.sum(squares[6:7], axis=1, keepdims=True)
 
 
 def exchange(
     place, send, parts_ref, chunk_ref, gathered_ref,
     from_core, sum_core, relay_up, relay_down, from_x, sum_x, from_y, sum_y, from_z, sum_z, got_z,
-    block, block_y, block_k,
+    head_z, block, block_y, block_k, square, square_y, part_square, square_k,
 ):
     nx, ny, nz = place.nx, place.ny, place.nz
     order = sorted(range(1, ny), key=lambda d: -min(d, ny - d)) + [0]
@@ -302,30 +299,45 @@
     wait_all(along)
     sum_y[TILES:nz] = jnp.zeros((nz - TILES, 8, 128), jnp.float32)
     sum_y[0:TILES] = total_of(sum_x[0], from_y, ny - 1)
-    wait_all(
-        [
-            send(sum_y.at[lax.rem(place.z + d, nz)], from_z.at[d - 1], place.along_z(d))
-            for d in range(1, nz)
-        ]
-    )
+    copies = [
+        send(sum_y.at[lax.rem(place.z + d, nz)], from_z.at[d - 1], place.along_z(d))
+        for d in range(1, nz)
+    ]
+    heads = [
+        send(sum_y.at[TILES - 1], head_z.at[d - 1], place.along_z(d)) for d in range(1, nz)
+    ]
+    wait_all(copies)
     sum_z[...] = total_of(sum_y[place.z], from_z, nz - 1)
     copies = [send(sum_z, got_z.at[d], place.along_z(d)) for d in range(1, nz)]
     chunk_ref[place.z] = sum_z[...]
+    wait_all(heads)
+    block[...] = total_of(sum_y[TILES - 1], head_z, nz - 1)
+    heads = [send(block, block_y.at[d], place.along_y(d)) for d in range(1, ny)]
+    block_y[0] = block[...]
+    wait_all(heads)
+    heads = [send(block_y, block_k.at[d], place.along_k(d)) for d in range(1, 2 * nx)]
+    block_k[0] = block_y[...]
     wait_all(copies)
     for d in range(1, nz):
         chunk_ref[lax.rem(place.z - d + nz, nz)] = got_z[d]
     conv = chunk_ref[0:9]
-    squares = jnp.sum(jnp.sum(conv * conv, axis=0), axis=0, keepdims=True)
-    block[...] = jnp.where(
-        row_index() == 6, jnp.broadcast_to(squares, (8, 128)), chunk_ref[TILES - 1]
-    )
-    copies = [send(block, block_y.at[d], place.along_y(d)) for d in range(1, ny)]
-    block_y[0] = block[...]
-    wait_all(copies)
-    copies = [send(block_y, block_k.at[d], place.along_k(d)) for d in range(1, 2 * nx)]
-    block_k[0] = block_y[...]
-    wait_all(copies)
+    square[...] = jnp.sum(conv * conv, axis=0)
+    squares = [send(square, square_y.at[d - 1], place.along_y(d)) for d in range(1, ny)]
+    wait_all(squares)
+    part_square[...] = total_of(square[...], square_y, ny - 1)
+    squares = [send(part_square, square_k.at[d - 1], place.along_k(d)) for d in range(1, 2 * nx)]
+    wait_all(heads)
     spread(place, block_k, gathered_ref)
+
+    def conv_norm():
+        wait_all(squares)
+        return sum_of(total_of(part_square[...], square_k, 2 * nx - 1))
+
+    return conv_norm
+
+
+def sum_of(array):
+    return jnp.sum(jnp.sum(array, axis=0, keepdims=True), axis=1, keepdims=True)
 
 
 def dot_highest(left, right):
@@ -335,23 +347,22 @@
 
 
 def updates(
-    place, samples_all, chunk_ref, gathered_ref, a_factor_ref, g_factor_ref, g_inverse_ref,
-    inverse_ref, head_ref, output_ref, precond_ref,
+    place, samples_all, conv_norm, chunk_ref, gathered_ref, a_factor_ref, g_factor_ref,
+    g_inverse_ref, inverse_ref, head_ref, output_ref, precond_ref,
     head_update_ref, conv_update_ref, new_a_ref, new_g_ref,
 ):
-    conv_norm = head_from(place.nx, place.ny, gathered_ref, head_ref, output_ref)
+    head_from(place.nx, place.ny, gathered_ref, head_ref, output_ref)
     head_grad = head_ref[...]
     precond = dot_highest(dot_highest(inverse_ref[...], head_grad), g_inverse_ref[...])
     precond_ref[...] = precond
-    head_norm = jnp.sum(
-        jnp.sum(precond * head_grad, axis=0, keepdims=True), axis=1, keepdims=True
-    )
+    head_norm = sum_of(precond * head_grad)
     head_scale = -jnp.sqrt(C * NE / 4.0 / head_norm)
-    conv_scale = -jnp.sqrt(9 * C * C / 4.0 / conv_norm)
     pair = pl.multiple_of(lax.div(place.orb, 2) * 8, 8)
     eight = head_scale * precond_ref[pl.ds(pair, 8), :]
     head_update_ref[...] = jnp.where(place.c == 0, eight, pltpu.roll(eight, 4, 0))[0:4]
     keep = 1.0 - decay_rate
+    new_g_ref[...] = decay_rate * g_factor_ref[...] + keep * output_ref[...] / samples_all
+    conv_scale = -jnp.sqrt(9 * C * C / 4.0 / conv_norm())
     for half in range(2):
         lanes = slice(128 * half, 128 * half + 128)
         rows = slice(4 * half, 4 * half + 4)
@@ -371,8 +382,6 @@
         def _(lanes=lanes, inner=inner, edge=edge):
             conv_update_ref[0:4, lanes] = edge
             conv_update_ref[4:36, lanes] = inner
-
-    new_g_ref[...] = decay_rate * g_factor_ref[...] + keep * output_ref[...] / samples_all
 
 
 def step_kernel(
@@ -455,9 +464,9 @@
     )
     lay_out(nx, ny, conv_ref, input_ref, head_ref, output_ref, parts_ref)
     wait_all(loads[6:])
-    exchange(place, send, parts_ref, chunk_ref, gathered_ref, *buffers)
+    conv_norm = exchange(place, send, parts_ref, chunk_ref, gathered_ref, *buffers)
     updates(
-        place, samples_all, chunk_ref, gathered_ref, a_factor_ref, g_factor_ref, g_inverse_ref,
+        place, samples_all, conv_norm, chunk_ref, gathered_ref, a_factor_ref, g_factor_ref, g_inverse_ref,
         inverse_ref, head_ref, output_ref, precond_ref,
         head_update_ref, conv_update_ref, new_a_ref, new_g_ref,
     )
@@ -481,7 +490,7 @@
     sites = L * L
     orb = 2 * nx * ny
     copies = 2 * (ny - 1) + 2 * (2 * nx - 1) + nz - 1
-    copies += 5 * ny + 2 * (ny - 1) + 2 * (nz - 1) + 2 * nx - 1
+    copies += 5 * ny + 3 * (ny - 1) + 3 * (nz - 1) + 2 * (2 * nx - 1)
 
     inputs = (
         occupations,
@@ -550,9 +559,14 @@
             tiles(nz - 1),
             tiles(),
             tiles(nz),
+            tiles(nz - 1),
             tiles(),
             tiles(ny),
             tiles(2 * nx, ny),
+            tiles(),
+            tiles(ny - 1),
+            tiles(),
+            tiles(2 * nx - 1),
             pltpu.SemaphoreType.DMA((len(inputs),)),
             pltpu.SemaphoreType.DMA((copies,)),
             pltpu.SemaphoreType.DMA((copies,)),

time: 87.2 us -> 86.3 us (0.990)
  Pallas kernels: 80.9 us -> 80 us
    pallas_call x1, Pallas kernels: 80.9 us -> 80 us  [per_device(): pl.pallas_call(functools.partial(step_kernel, nx, ny, nz, samples), name=...]
where the time goes in v4:
time: 86.3 us; the launch traced here: 86 us
  Pallas kernels  80 us (93%)
  local copies, waits for them, and re-layouts  5.4 us (6%)
    pallas_call x1, Pallas kernels, per_device(): pl.pallas_call(functools.partial(step_kernel, nx, ny, nz, samples), name=...  80 us
    unnamed x4, local copies, waits for them, and re-layouts  5.4 us

profile of v4, /device:TPU:1, one launch (start us, length us, event | category | flops | bytes accessed | tf_op | source)
XLA Modules:
  0.0 86.0 jit_solution(6644376869923322843)
XLA Ops:
  0.6 80.0 %natural_step.1 = (f32[4,128]{1,0:T(4,128)}, f32[36,256]{1,0:T(8,128)}, f32[4,256]{1,0:T(4,128)}, f32[128,128]{1,0:T(8,128)}) custom-call(s32[4,128]{1,0:T(4,128)} %occ_in.1, f32[1,4]{1,0:T(1,128)} %bitcast.1, f32[4,256]{1,0:T(4,128)} %a_inverse_in.1, bf16[18,256]{1,0:T(8,128)(2,1)} %embed_in.1, bf16[2304,256]{1,0:T(8,128)(2,1)} %conv_w_in.1, ...), custom_call_target="tpu_custom_call" | custom-call | tf_op jit(solution)/shard_map/natural_step/pallas_call | solution.py:513
  80.6 1.3 %copy.17 = f32[4,128]{1,0:T(4,128)} copy(f32[4,128]{1,0:T(4,128)} %get-tuple-element.8) | data formatting | bytes 4096
  81.9 1.4 %copy.18 = f32[36,256]{1,0:T(8,128)} copy(f32[36,256]{1,0:T(8,128)} %get-tuple-element.9) | data formatting | bytes 73728
  83.3 1.3 %copy.19 = f32[4,256]{1,0:T(4,128)} copy(f32[4,256]{1,0:T(4,128)} %get-tuple-element.10) | data formatting | bytes 8192
  84.5 1.5 %copy.20 = f32[128,128]{1,0:T(8,128)} copy(f32[128,128]{1,0:T(8,128)} %get-tuple-element.11) | data formatting | bytes 131072

commit v5 on v4

--- a/solution.py
+++ b/solution.py
@@ -206,7 +206,7 @@
             conv_ref[rows, :] = term if b == 0 else conv_ref[rows, :] + term
 
 
-def lay_out(nx, ny, conv_ref, input_ref, head_ref, output_ref, parts_ref):
+def lay_out(nx, ny, conv_ref, input_ref, head_ref, output_ref, parts_ref, ready):
     row = lax.broadcasted_iota(jnp.int32, (8, 128), 0)
 
     def halves(first, second, c):
@@ -214,8 +214,8 @@
             return jnp.where(row < 4, first, pltpu.roll(second, 4, 0))
         return jnp.where(row < 4, pltpu.roll(first, 4, 0), second)
 
-    for pair in range(nx * ny):
-        x, y = pair // ny, pair % ny
+    for y, x in [(y, x) for y in range(ny) for x in range(nx)]:
+        pair = x * ny + y
         for c in range(2):
             top = 72 * pair + 40 * c
             for half in range(2):
@@ -232,6 +232,8 @@
             output = pltpu.roll(output, (4 - place) % 8, 0) if place != 4 else output
             head = head_ref[eight, :] if c == 0 else pltpu.roll(head_ref[eight, :], 4, 0)
             parts_ref[c, x, y, 10] = jnp.where(row < 4, head, output)
+        if x == nx - 1:
+            ready(y)
 
 
 def row_index():
@@ -263,7 +265,7 @@
 
 
 def exchange(
-    place, send, parts_ref, chunk_ref, gathered_ref,
+    place, send, core, parts_ref, chunk_ref, gathered_ref,
     from_core, sum_core, relay_up, relay_down, from_x, sum_x, from_y, sum_y, from_z, sum_z, got_z,
     head_z, block, block_y, block_k, square, square_y, part_square, square_k,
 ):
@@ -272,12 +274,9 @@
     at_x = [lax.rem(place.x + d, nx) for d in range(nx)]
     at_y = [lax.rem(place.y + d, ny) for d in range(ny)]
     low, high = pl.ds(0, HALF), pl.ds(HALF, TILES - HALF)
-    core, relays, across, along = {}, {}, {}, []
+    relays, across, along = {}, {}, []
+    wait_all(core)
     for d in order:
-        source = parts_ref.at[1 - place.c, :, at_y[d]]
-        core[d] = send(source, from_core.at[:, at_y[d]], place.core())
-    for d in order:
-        core[d].wait()
         sum_core[:, at_y[d]] = parts_ref[place.c, :, at_y[d]] + from_core[:, at_y[d]]
         relays[d] = [
             send(sum_core.at[at_x[2], at_y[d], low], relay_up.at[d], place.along_x(1)),
@@ -462,9 +461,15 @@
         lambda b: (energy_of(b)[0:1] - mean_energy) / samples_all,
         embedded_ref, pre_ref, rows_t_ref, cot_ref, conv_ref, head_ref,
     )
-    lay_out(nx, ny, conv_ref, input_ref, head_ref, output_ref, parts_ref)
+    core = []
+
+    def send_core(y):
+        source, target = parts_ref.at[1 - place.c, :, y], buffers[0].at[:, y]
+        core.append(send(source, target, place.core()))
+
+    lay_out(nx, ny, conv_ref, input_ref, head_ref, output_ref, parts_ref, send_core)
     wait_all(loads[6:])
-    conv_norm = exchange(place, send, parts_ref, chunk_ref, gathered_ref, *buffers)
+    conv_norm = exchange(place, send, core, parts_ref, chunk_ref, gathered_ref, *buffers)
     updates(
         place, samples_all, conv_norm, chunk_ref, gathered_ref, a_factor_ref, g_factor_ref, g_inverse_ref,
         inverse_ref, head_ref, output_ref, precond_ref,

time: 86.3 us -> 88.1 us (1.021)
  Pallas kernels: 80 us -> 81.7 us
    pallas_call x1, Pallas kernels: 80 us -> 81.7 us  [per_device(): pl.pallas_call(functools.partial(step_kernel, nx, ny, nz, samples), name=...]
where the time goes in v5:
time: 88.1 us; the launch traced here: 87.7 us
  Pallas kernels  81.7 us (93%)
  local copies, waits for them, and re-layouts  5.4 us (6%)
    pallas_call x1, Pallas kernels, per_device(): pl.pallas_call(functools.partial(step_kernel, nx, ny, nz, samples), name=...  81.7 us
    unnamed x4, local copies, waits for them, and re-layouts  5.4 us

profile of v5, /device:TPU:1, one launch (start us, length us, event | category | flops | bytes accessed | tf_op | source)
XLA Modules:
  0.0 87.7 jit_solution(13146471172535318714)
XLA Ops:
  0.6 81.7 %natural_step.1 = (f32[4,128]{1,0:T(4,128)}, f32[36,256]{1,0:T(8,128)}, f32[4,256]{1,0:T(4,128)}, f32[128,128]{1,0:T(8,128)}) custom-call(s32[4,128]{1,0:T(4,128)} %occ_in.1, f32[1,4]{1,0:T(1,128)} %bitcast.1, f32[4,256]{1,0:T(4,128)} %a_inverse_in.1, bf16[18,256]{1,0:T(8,128)(2,1)} %embed_in.1, bf16[2304,256]{1,0:T(8,128)(2,1)} %conv_w_in.1, ...), custom_call_target="tpu_custom_call" | custom-call | tf_op jit(solution)/shard_map/natural_step/pallas_call | solution.py:518
  82.3 1.3 %copy.17 = f32[4,128]{1,0:T(4,128)} copy(f32[4,128]{1,0:T(4,128)} %get-tuple-element.8) | data formatting | bytes 4096
  83.6 1.4 %copy.18 = f32[36,256]{1,0:T(8,128)} copy(f32[36,256]{1,0:T(8,128)} %get-tuple-element.9) | data formatting | bytes 73728
  85.0 1.3 %copy.19 = f32[4,256]{1,0:T(4,128)} copy(f32[4,256]{1,0:T(4,128)} %get-tuple-element.10) | data formatting | bytes 8192
  86.3 1.5 %copy.20 = f32[128,128]{1,0:T(8,128)} copy(f32[128,128]{1,0:T(8,128)} %get-tuple-element.11) | data formatting | bytes 131072
